TPU v7x, 256 devices: a whole 4x4x8 slice. The times are simulated.
256 devices in a mesh: order: 64 (over z, x, core), lat: 4 (over y).
Axes of the slice: x: 4, y: 4, z: 8, core: 2. Of those that a mesh axis runs over, the one named last changes fastest.
Arguments:
- position: float32 [128, 2, 64, 2160], P('order', None, None, 'lat'), may hold values from -6 to 6
- residual: float32 [128, 2, 64, 2160], P('order', None, None, 'lat'), as said below
- direction: float32 [128, 2, 64, 2160], P('order', None, None, 'lat'), as said below
- legendre: float32 [128, 2160, 2048], P('order', None, 'lat'), may hold values from -0.125 to 0.125
- order_of: int32 [128], replicated, may hold values from 0 to 2032, as said below
- class_idx: int32 [2048, 4320], P(('lat', 'order')), may hold values from 0 to 15
- land: int32 [2048, 4320], P(('lat', 'order')), may hold values 0 or 1
- class_weight: float32 [16, 2], replicated, may hold values from 0.2 to 5
- damping: float32 [2160], P('lat'), may hold values from 0.05 to 0.5
Outputs:
- new_position: float32 [128, 2, 64, 2160], P('order', None, None, 'lat')
- new_residual: float32 [128, 2, 64, 2160], P('order', None, None, 'lat')
- new_direction: float32 [128, 2, 64, 2160], P('order', None, None, 'lat')
Inputs may be any that keep to these rules, and one draw needn't show every extreme that they name: `order_of`: distinct multiples of 16: each of 0, 16, ..., 16 * (128 - 1) appears exactly once. `residual`: real-valued and not zero. `direction`: real-valued and not zero.
All inputs are finite; a program needn't handle non-finite values. No bound on the sum of `land` on one device may be relied on, other than what follows from the above.
Results may differ from a plain program's by a relative error of at most 0.000058.
Values sent between devices are 32-bit elements; how exact they have to be, the bound alone decides.
A program may use at most 128 MiB of HBM per device.

v0:
```python
import math

import jax
import jax.numpy as jnp
from jax import lax
from jax.sharding import PartitionSpec as P


def tables(order_of, longitudes):
    longitude = jnp.arange(longitudes, dtype=jnp.int32)
    phases = order_of[:, None] * longitude[None, :] % longitudes
    angles = phases.astype(jnp.float32) * (2.0 * math.pi / longitudes)
    return jnp.stack([jnp.cos(angles), jnp.sin(angles)])


def sample_sums(product):
    return jnp.sum(product, axis=(0, 1, 3))


def shards(
    position, residual, direction, legendre, order_of, class_idx, land, class_weight, damping
):
    highest = lax.Precision.HIGHEST
    m_local = position.shape[0]
    samples = position.shape[2]
    deg_local = position.shape[3]
    band_rows = legendre.shape[2]
    lat_index = lax.axis_index("lat")
    order_index = lax.axis_index("order")
    my_orders = lax.dynamic_slice_in_dim(order_of, order_index * m_local, m_local)
    deg_start = lat_index * deg_local
    own_degrees = deg_start + jnp.arange(deg_local, dtype=jnp.int32)
    own_valid = (own_degrees[None, :] >= my_orders[:, None]).astype(jnp.float32)[:, None, None, :]
    pos_m = position * own_valid
    res_m = residual * own_valid
    dir_m = direction * own_valid
    norm_before = lax.psum(sample_sums(res_m * res_m), ("order", "lat"))
    block_part = lax.all_gather(direction, "lat", axis=3, tiled=True)
    degree_count = block_part.shape[3]
    in_block = jnp.arange(degree_count, dtype=jnp.int32)
    in_triangle = (in_block[None, :] >= my_orders[:, None]).astype(jnp.float32)
    masked = block_part * in_triangle[:, None, None, :]
    synthesis = jnp.einsum("mskd,mdt->mtsk", masked, legendre, precision=highest)
    grid_in = lax.all_to_all(
        synthesis.reshape(m_local, band_rows, 2 * samples),
        "order",
        split_axis=1,
        concat_axis=0,
        tiled=True,
    )
    orders_all = grid_in.shape[0]
    rows_here = grid_in.shape[1]
    grid_in = grid_in.reshape(orders_all, rows_here, 2, samples)
    longitudes = class_idx.shape[1]
    harmonic = tables(order_of, longitudes)
    surface = jnp.einsum("mrsk,sml->rkl", grid_in, harmonic, precision=highest)
    class_count = class_weight.shape[0]
    onehot = (
        class_idx[:, :, None] == jnp.arange(class_count, dtype=jnp.int32)[None, None, :]
    ).astype(jnp.float32)
    by_class = jnp.dot(onehot, class_weight, precision=highest)
    weight_grid = jnp.where(land == 1, by_class[:, :, 1], by_class[:, :, 0])
    weighted = surface * weight_grid[:, None, :]
    spectra = jnp.einsum("rkl,sml->mrsk", weighted, harmonic, precision=highest) * (
        2.0 / longitudes
    )
    returned = lax.all_to_all(
        spectra.reshape(orders_all, rows_here, 2 * samples),
        "order",
        split_axis=0,
        concat_axis=1,
        tiled=True,
    )
    returned = returned.reshape(m_local, band_rows, 2, samples)
    band_part = jnp.einsum("mtsk,mdt->mskd", returned, legendre, precision=highest)
    totals = lax.psum(band_part, "lat")
    summed = lax.dynamic_slice_in_dim(totals, deg_start, deg_local, 3)
    applied = (summed + damping[None, None, None, :] * dir_m) * own_valid
    curvature_sum = lax.psum(sample_sums(dir_m * applied), ("order", "lat"))
    step_size = (norm_before / curvature_sum)[None, None, :, None]
    new_residual = res_m - step_size * applied
    norm_after = lax.psum(sample_sums(new_residual * new_residual), ("order", "lat"))
    ratio_new = (norm_after / norm_before)[None, None, :, None]
    new_position = pos_m + step_size * dir_m
    new_direction = new_residual + ratio_new * dir_m
    return (new_position, new_residual, new_direction)


def solution(mesh):
    return jax.shard_map(
        shards,
        mesh=mesh,
        in_specs=(
            P("order", None, None, "lat"),
            P("order", None, None, "lat"),
            P("order", None, None, "lat"),
            P("order", None, "lat"),
            P(),
            P(("lat", "order"), None),
            P(("lat", "order"), None),
            P(),
            P("lat"),
        ),
        out_specs=(
            P("order", None, None, "lat"),
            P("order", None, None, "lat"),
            P("order", None, None, "lat"),
        ),
        check_vma=False,
    )
```

profile of v0, /device:TPU:1, one launch (start us, length us, event | category | flops | bytes accessed | tf_op | source)
XLA Modules:
  0.0 420.0 jit_solution(14200132624685688203)
XLA Ops:
  7.2 2.3 copy.20
  9.7 0.7 fusion.11
  10.6 0.9 fusion.37
  11.4 9.9 %fusion.17 = (f32[1,128,4320]{1,2,0:T(8,128)S(1)}, f32[1,128,4320]{1,2,0:T(8,128)}) fusion(s32[128]{0:T(128)S(1)} %copy-done.10), kind=kLoop, calls=%fused_computation.23 | loop fusion | flops 4976640 | bytes 4424192 | tf_op jit(solution)/shard_map/cos | solution.py:13
  21.3 44.9 %all-gather.2.cloned.1.call-done = f32[2,2,64,2160]{2,1,0,3:T(2,128)} async-done(((f32[2,2,64,540]{2,1,0,3:T(2,128)}), f32[2,2,64,2160]{2,1,0,3:T(2,128)}) %all-gather.2.cloned.1.call-update) | async-done | bytes 2211856 | tf_op jit(solution)/shard_map/all_gather | solution.py:38
  66.2 6.6 %broadcast_multiply_fusion = f32[2,2,64,2160]{2,1,0,3:T(2,128)S(1)} fusion(f32[2,2,64,2160]{2,1,0,3:T(2,128)} %all-gather.2.cloned.1.call-done, f32[2,2160]{0,1:T(8,128)S(1)} %fusion.30), kind=kLoop, calls=%fused_computation.18 | loop fusion | flops 552960 | bytes 4440960 | tf_op jit(solution)/shard_map/mul | solution.py:42
  72.8 8.7 %fusion.4 = f32[2,2,64,512]{3,2,1,0:T(8,128)S(1)} fusion(f32[2,2160,512]{2,1,0:T(8,128)S(1)} %copy-done.1, f32[2,2,64,2160]{2,1,0,3:T(2,128)S(1)} %broadcast_multiply_fusion), kind=kOutput, calls=%fused_computation.5 | convolution fusion | flops 3397386240 | bytes 11583488 | tf_op jit(solution)/shard_map/mskd,mdt->mtsk/dot_general | solution.py:43
  81.5 1.0 copy.22
  82.5 10.8 %all-to-all-start = ((f32[2,512,128]{2,0,1:T(2,128)}), f32[2,512,128]{2,0,1:T(2,128)S(1)}, u32[]{:S(2)}, u32[]{:S(2)}) async-start(f32[2,512,128]{2,0,1:T(2,128)} %copy.22), calls=%async_computation | async-start | bytes 1048576 | tf_op jit(solution)/shard_map/all_to_all | solution.py:44
  93.3 0.5 all-reduce.3.cloned.1.call-start
  93.9 17.1 %all-to-all-done = f32[2,512,128]{2,0,1:T(2,128)S(1)} async-done(((f32[2,512,128]{2,0,1:T(2,128)}), f32[2,512,128]{2,0,1:T(2,128)S(1)}, u32[]{:S(2)}, u32[]{:S(2)}) %all-to-all-start) | async-done | bytes 524320 | tf_op jit(solution)/shard_map/all_to_all | solution.py:44
  111.0 0.8 copy.24
  111.9 1.6 reshape.148
  113.5 31.0 %fusion.8 = f32[8,64,4320,1]{2,1,3,0:T(8,128)S(1)} fusion(f32[1,128,4320]{1,2,0:T(8,128)} %get-tuple-element.13, f32[1,128,4320]{1,2,0:T(8,128)S(1)} %get-tuple-element.12, f32[128,8,2,64]{3,2,1,0:T(2,128)S(1)} %reshape.148), kind=kOutput, calls=%fused_computation.10 | convolution fusion | flops 6795878400 | bytes 13795328 | tf_op jit(solution)/shard_map/mrsk,sml->rkl/dot_general | solution.py:56
  144.6 7.8 %fusion.24 = f32[128,8,2,64]{0,3,1,2:T(8,128)S(1)} fusion(f32[8,64,4320,1]{2,1,3,0:T(8,128)S(1)} %fusion.8, f32[8,4320]{1,0:T(8,128)S(1)} %fusion.33, f32[1,128,4320]{1,2,0:T(8,128)S(1)} %copy-done.2, f32[1,128,4320]{1,2,0:T(8,128)S(1)} %get-tuple-element.12), kind=kOutput, calls=%fused_computation.26 | convolution fusion | flops 6798221312 | bytes 13933568 | tf_op jit(solution)/shard_map/rkl,sml->mrsk/dot_general | solution.py:64
  152.7 23.4 %all_to_all.30 = f32[128,8,128]{2,1,0:T(8,128)S(1)} all-to-all(f32[128,8,128]{2,1,0:T(8,128)S(1)} %copy.28), channel_id=1, replica_groups=mesh['order'=64,'lat'=4] {'order'}, dimensions={0} | all-to-all | bytes 1048576 | tf_op jit(solution)/shard_map/all_to_all | solution.py:67
  176.2 0.6 reshape.150
  176.8 19.2 %fusion.2 = f32[2,2,64,2160]{3,2,1,0:T(8,128)} fusion(f32[2,2160,512]{2,1,0:T(8,128)} %param.12, f32[2,512,2,64]{3,2,1,0:T(2,128)S(1)} %reshape.150), kind=kOutput, calls=%fused_computation.3 | convolution fusion | flops 3397386240 | bytes 11583488 | tf_op jit(solution)/shard_map/mtsk,mdt->mskd/dot_general | solution.py:75
  196.2 61.3 %all-reduce.3.cloned.1.call-done = f32[2,2,64,2160]{3,2,1,0:T(8,128)} async-done(((f32[2,2,64,2160]{3,2,1,0:T(8,128)}), f32[2,2,64,2160]{3,2,1,0:T(8,128)}) %all-reduce.3.cloned.1.call-update) | async-done | bytes 2211856 | tf_op jit(solution)/shard_map/psum | solution.py:76
  257.4 1.6 multiply_reduce_fusion.1
  259.0 76.0 %all-reduce = (f32[64]{0:T(128)S(1)}, f32[64]{0:T(128)S(1)}) all-reduce(f32[64]{0:T(128)S(1)} %get-tuple-element.4, f32[64]{0:T(128)S(1)} %get-tuple-element.3), channel_id=1, replica_groups=mesh['order'=64,'lat'=4] {'order','lat'}, use_global_device_ids=true, to_apply=%region_1.0 | all-reduce | flops 128 | bytes 1024 | tf_op jit(solution)/shard_map/psum | solution.py:37
  335.0 2.5 multiply_reduce_fusion
  337.5 74.3 %psum.31 = f32[64]{0:T(128)S(1)} all-reduce(f32[64]{0:T(128)S(1)} %get-tuple-element.7), channel_id=1, replica_groups=mesh['order'=64,'lat'=4] {'order','lat'}, use_global_device_ids=true, to_apply=%region_6.7 | all-reduce | flops 64 | bytes 512 | tf_op jit(solution)/shard_map/psum | solution.py:82
  411.8 1.0 multiply_add_fusion
  (38 shorter events, 0.8 us)
Async XLA Ops:
  7.2 2.5 copy-start
  7.2 2.4 copy-start.10
  7.2 2.5 copy-start.11
  7.2 59.0 %all-gather.2.cloned.1.call-start = ((), (), s32[]{:S(2)}) async-start(), calls=%async_computation.2 | async-start | bytes 5529600 | tf_op jit(solution)/shard_map/all_gather | solution.py:38
  66.2 6.6 %copy-start.1 = (f32[2,2160,512]{2,1,0:T(8,128)S(1)}, f32[2,2160,512]{2,1,0:T(8,128)}, u32[]{:S(2)}) copy-start(f32[2,2160,512]{2,1,0:T(8,128)} %param.12) | copy-start | bytes 26542084
  72.7 21.1 %copy-start.7 = (f32[8,4320,1]{1,2,0:T(1,128)S(1)}, f32[8,4320,1]{1,2,0:T(1,128)}, u32[]{:S(2)}) copy-start(f32[8,4320,1]{1,2,0:T(1,128)} %get-tuple-element.11) | copy-start | bytes 414724
  72.8 21.1 %copy-start.8 = (s32[8,4320]{1,0:T(8,128)S(1)}, s32[8,4320]{1,0:T(8,128)}, u32[]{:S(2)}) copy-start(s32[8,4320]{1,0:T(8,128)} %param.15) | copy-start | bytes 414724
  82.5 28.5 %all-to-all-start = ((f32[2,512,128]{2,0,1:T(2,128)}), f32[2,512,128]{2,0,1:T(2,128)S(1)}, u32[]{:S(2)}, u32[]{:S(2)}) async-start(f32[2,512,128]{2,0,1:T(2,128)} %copy.22), calls=%async_computation | async-start | bytes 1048576 | tf_op jit(solution)/shard_map/all_to_all | solution.py:44
  93.3 164.1 %all-reduce.3.cloned.1.call-start = ((), (), s32[]{:S(2)}) async-start(), calls=%async_computation.3 | async-start | bytes 4456448 | tf_op jit(solution)/shard_map/psum | solution.py:76
  113.5 31.1 %copy-start.2 = (f32[1,128,4320]{1,2,0:T(8,128)S(1)}, f32[1,128,4320]{1,2,0:T(8,128)}, u32[]{:S(2)}) copy-start(f32[1,128,4320]{1,2,0:T(8,128)} %get-tuple-element.13) | copy-start | bytes 6635524
  196.0 61.4 %copy-start.3 = (f32[2,2,64,540]{3,2,1,0:T(8,128)S(1)}, f32[2,2,64,540]{3,2,1,0:T(8,128)}, u32[]{:S(2)}) copy-start(f32[2,2,64,540]{3,2,1,0:T(8,128)} %param.11) | copy-start | bytes 1658884
  196.0 61.4 %copy-start.4 = (f32[2,2,64,540]{3,2,1,0:T(8,128)S(1)}, f32[2,2,64,540]{3,2,1,0:T(8,128)}, u32[]{:S(2)}) copy-start(f32[2,2,64,540]{3,2,1,0:T(8,128)} %param.10) | copy-start | bytes 1658884
  196.0 61.4 %copy-start.9 = (f32[540]{0:T(1024)S(1)}, f32[540]{0:T(1024)}, u32[]{:S(2)}) copy-start(f32[540]{0:T(1024)} %param.17) | copy-start | bytes 6484
  196.0 138.9 %copy-start.6 = (f32[2,2,64,540]{3,2,1,0:T(8,128)S(1)}, f32[2,2,64,540]{3,2,1,0:T(8,128)}, u32[]{:S(2)}) copy-start(f32[2,2,64,540]{3,2,1,0:T(8,128)} %param.9) | copy-start | bytes 1658884
  337.4 75.3 %copy-start.5 = (f32[2,2,64,540]{3,2,1,0:T(8,128)}, f32[2,2,64,540]{3,2,1,0:T(8,128)S(1)}, u32[]{:S(2)}) copy-start(f32[2,2,64,540]{3,2,1,0:T(8,128)S(1)} %get-tuple-element.8) | copy-start | bytes 1658884
Sparse Core Ops, SparseCore 0:
  9.8 56.2 all-gather.1
  196.2 61.1 all-reduce.2
where the time goes:
time: 429 us; the launch traced here: 420 us
  blocking collectives  174 us (41%)
  waiting for transfers between devices  123 us (29%)
  matrix products  67.5 us (16%)
  other arithmetic  21.7 us (5%)
  between operations  14.7 us (3%)
  starting transfers between devices  11.4 us (3%)
  local copies, waits for them, and re-layouts  7.76 us (2%)
    psum x1, blocking collectives, shards(): norm_before = lax.psum(sample_sums(res_m * res_m), ('order', 'lat'))  76 us
    psum x1, blocking collectives, shards(): lax.psum(sample_sums(new_residual * new_residual), ('order', 'lat'))  74.3 us
    psum x1, waiting for transfers between devices, shards(): totals = lax.psum(band_part, 'lat')  61.3 us
    all_gather x1, waiting for transfers between devices, shards(): block_part = lax.all_gather(direction, 'lat', axis=3, tiled=True)  44.9 us
    dot_general x1, matrix products, shards(): surface = jnp.einsum('mrsk,sml->rkl', grid_in, harmonic, precision=highest)  31 us
    all_to_all x1, blocking collectives, shards(): lax.all_to_all(spectra.reshape(orders_all, rows_here, 2 * samples), 'orde...  23.4 us
    dot_general x1, matrix products, shards(): jnp.einsum('mtsk,mdt->mskd', returned, legendre, precision=highest)  19.2 us
    all_to_all x1, waiting for transfers between devices, shards(): lax.all_to_all(synthesis.reshape(m_local, band_rows, 2 * samples), 'order...  17.1 us
  transfers between devices with their start and end apart: 3, of which 3 were waited for; matrix products, arithmetic and copies ran while one was open for 3% of the time, Pallas kernels for 0%

commit v1 on v0

v1 whole, which is shorter than its diff:
```python
import functools
import math

import jax
import jax.numpy as jnp
from jax import lax
from jax.experimental import pallas as pl
from jax.experimental.pallas import tpu as pltpu
from jax.sharding import PartitionSpec as P

F32 = jnp.float32
BF16 = jnp.bfloat16
MESH = pl.DeviceIdType.MESH

NO = 64
NL = 4
DEG = 540
SLOT = 544
HALF = SLOT // 2
WIDE = 640
STARTS = (0, 536, 1080, 1616)
BAND = 512
CH = 2
KC = 32
PERIOD = 270
NLON = 4320
ROWS_J = 272


def tall_to_wide(x):
    n = x.shape[0] // 128
    return jnp.concatenate([x[128 * i : 128 * (i + 1)].T for i in range(n)], axis=1)


def wide_to_tall(x):
    n = x.shape[1] // 128
    return jnp.concatenate([x[:, 128 * i : 128 * (i + 1)].T for i in range(n)], axis=0)


def split(x):
    hi = x.astype(BF16)
    lo = (x - hi.astype(F32)).astype(BF16)
    return hi, lo


def mm(a, b):
    return jnp.dot(a, b, preferred_element_type=F32)


def iota(shape, axis):
    return lax.broadcasted_iota(jnp.int32, shape, axis)


def fold4(x):
    y = x + pltpu.roll(x, 64, 1)
    return y + pltpu.roll(y, 32, 1)


def row_sum(x):
    acc = x[:, 0:128]
    for i in range(1, WIDE // 128):
        acc = acc + x[:, 128 * i : 128 * (i + 1)]
    return jnp.sum(acc.T, axis=0, keepdims=True)


def column(row):
    return jnp.broadcast_to(row, (128, 128)).T


def kernel(
    pos_h, res_h, dir_h, leg_h, cls_h, land_h, order_s, order_v, cw_s, damp_v,
    npos_h, nres_h, ndir_h,
    lf, lh, ll, dir_v, res_v, pos_v, cls_v, land_v, wv,
    dn, dampp, g, sy, r, t, q, pp, ra, rb, v1, v2, nres_v,
    hth, htl, hh, hl, wx, rs_acc,
    lsem, isem, osem, ag_s, ag_r, a2_s, a2_r, b2_s, b2_r, rs_s, rs_r, v1_s, v1_r, v2_s, v2_r,
):
    o = lax.axis_index("order")
    l = lax.axis_index("lat")
    right = lax.rem(l + 1, NL)
    left = lax.rem(l + NL - 1, NL)
    opp = lax.rem(l + 2, NL)
    odd = lax.rem(l, 2)

    in_dir = pltpu.make_async_copy(dir_h, dir_v, isem.at[0])
    in_dir.start()
    leg_in = []
    for b in range(NL):
        for m in range(2):
            c = pltpu.make_async_copy(
                leg_h.at[m, pl.ds(STARTS[b], SLOT), :], lf.at[m, b], lsem.at[2 * b + m]
            )
            c.start()
            leg_in.append(c)
    in_res = pltpu.make_async_copy(res_h, res_v, isem.at[1])
    in_pos = pltpu.make_async_copy(pos_h, pos_v, isem.at[2])
    in_cls = pltpu.make_async_copy(cls_h, cls_v, isem.at[3])
    in_land = pltpu.make_async_copy(land_h, land_v, isem.at[4])
    for c in (in_res, in_pos, in_cls, in_land):
        c.start()

    barrier = pltpu.get_barrier_semaphore()

    def greet(i, carry):
        peer = lax.rem(o + i, NO)
        pl.semaphore_signal(barrier, inc=1, device_id=(peer, l), device_id_type=MESH)
        return carry

    for i in range(1, NL):
        pl.semaphore_signal(
            barrier, inc=1, device_id=(o, lax.rem(l + i, NL)), device_id_type=MESH
        )
    lax.fori_loop(1, NO, greet, 0)

    row = iota((128, WIDE), 0)
    lane = iota((128, WIDE), 1)
    order_row = jnp.where(row < 64, order_s[2 * o], order_s[2 * o + 1])
    valid = (lane < DEG) & (lane + l * DEG >= order_row)

    def natural(ref, c):
        return jnp.concatenate(
            [ref[m, s, c * KC : (c + 1) * KC, :] for m in range(2) for s in range(2)],
            axis=0,
        )

    in_dir.wait()
    for c in range(CH):
        dn[c, :, 512:WIDE] = jnp.zeros((128, 128), F32)
        dn[c, :, 0:DEG] = natural(dir_v, c)
        x = jnp.where(valid, dn[c], 0.0)
        dn[c] = x
        shifted = jnp.where(odd == 1, pltpu.roll(x, 4, 1), x)
        g[c, l] = wide_to_tall(shifted)[0:SLOT]

    pl.semaphore_wait(barrier, NO - 1 + NL - 1)

    def ag(c, k, slot, lo, to):
        return pltpu.make_async_remote_copy(
            src_ref=g.at[c, slot, pl.ds(lo, HALF), :],
            dst_ref=g.at[c, slot, pl.ds(lo, HALF), :],
            send_sem=ag_s.at[c, k],
            recv_sem=ag_r.at[c, k],
            device_id=(o, to),
            device_id_type=MESH,
        )

    def ag_first(c):
        ag(c, 0, l, 0, right).start()
        ag(c, 1, l, HALF, left).start()
        ag(c, 2, l, HALF, right).start()
        ag(c, 3, l, 0, left).start()

    def ag_forward(c):
        ag(c, 0, left, 0, right).wait_recv()
        ag(c, 4, left, 0, right).start()
        ag(c, 1, right, HALF, left).wait_recv()
        ag(c, 5, right, HALF, left).start()

    ag_first(0)

    def convert(b, m):
        leg_in[2 * b + m].wait()

        def body(i, carry):
            at = pl.ds(pl.multiple_of(i * 32, 32), 32)
            hi, lo = split(lf[m, b, at, :])
            lh[m, b, at, :] = hi
            ll[m, b, at, :] = lo
            return carry

        lax.fori_loop(0, SLOT // 32, body, 0)

    for b in range(NL // 2):
        for m in range(2):
            convert(b, m)

    ag_forward(0)
    ag_first(1)

    for b in range(NL // 2, NL):
        for m in range(2):
            convert(b, m)

    col = iota((128, 256), 1)
    pick = (iota((128, 256), 0) == 2 * (col & 63) + (col >> 7)).astype(F32)
    sixteenth = jnp.broadcast_to(order_v[...].astype(F32) * (1.0 / 16.0), (8, 128))
    orders = mm(sixteenth.astype(BF16), pick.astype(BF16))[0:1, :] * 16.0
    j = iota((384, 256), 0).astype(F32)
    turns = j * orders
    phase = turns - jnp.floor(turns * (1.0 / NLON)) * float(NLON)
    part = (iota((384, 256), 1) >> 6) & 1
    phase = phase - jnp.where(part == 1, float(NLON // 4), 0.0)
    table = jnp.cos(phase * (2.0 * math.pi / NLON))
    hi, lo = split(table)
    hth[...] = hi[0:ROWS_J]
    htl[...] = lo[0:ROWS_J]
    flat = jnp.concatenate([tall_to_wide(table[:, 0:128]), tall_to_wide(table[:, 128:256])], 0)
    hi, lo = split(flat)
    hh[...] = hi[:, 0:ROWS_J]
    hl[...] = lo[:, 0:ROWS_J]

    in_cls.wait()
    in_land.wait()
    wv[:, 4224:4608] = jnp.zeros((8, 384), F32)
    for lo_lane in range(0, NLON, 640):
        n = min(640, NLON - lo_lane)
        cls = cls_v[:, lo_lane : lo_lane + n]
        on_land = land_v[:, lo_lane : lo_lane + n] == 1
        w = jnp.zeros((8, n), F32)
        for k in range(16):
            w = jnp.where(cls == k, jnp.where(on_land, cw_s[k, 1], cw_s[k, 0]), w)
        wv[:, lo_lane : lo_lane + n] = w
    folded = jnp.zeros((8, 512), F32)
    for i in range(NLON // PERIOD):
        base = PERIOD * i // 128 * 128
        off = PERIOD * i - base
        v = wv[:, base : base + 512]
        if off:
            v = pltpu.roll(v, 512 - off, 1)
        folded = folded + v
    folded = jnp.where(iota((8, 512), 1) < PERIOD, folded, 0.0) * (2.0 / NLON)
    folded = jnp.concatenate([folded[:, 0:384], jnp.zeros((120, 384), F32)], axis=0)
    spread = (iota((128, 256), 0) == (iota((128, 256), 1) >> 5)).astype(F32)
    wx[...] = jnp.dot(
        wide_to_tall(folded), spread, precision=lax.Precision.HIGHEST, preferred_element_type=F32
    )[0:ROWS_J]

    dampp[:, 512:WIDE] = jnp.zeros((1, 128), F32)
    dampp[:, 0:DEG] = damp_v[...]

    in_res.wait()
    norm_before = []
    damped = []
    for c in range(CH):
        nres_v[c, :, 512:WIDE] = jnp.zeros((128, 128), F32)
        nres_v[c, :, 0:DEG] = natural(res_v, c)
        x = jnp.where(valid, nres_v[c], 0.0)
        nres_v[c] = x
        norm_before.append(row_sum(x * x))
        y = dn[c]
        damped.append(row_sum(y * (y * dampp[...])))

    def synth(c, slot, first):
        x = jnp.concatenate([g[c, slot], jnp.zeros((WIDE - SLOT, 128), F32)], axis=0)
        wide = tall_to_wide(x)[:, 0:SLOT]
        hi, lo = split(wide)
        for m in range(2):
            a = 64 * m
            both = mm(
                jnp.concatenate([hi[a : a + 64], lo[a : a + 64]], axis=0), lh[m, slot]
            )
            out = both[0:64] + both[64:128] + mm(hi[a : a + 64], ll[m, slot])
            if first:
                rs_acc[a : a + 64, :] = out
            else:
                rs_acc[a : a + 64, :] = rs_acc[a : a + 64, :] + out

    def all_to_all(src, dst, c, ssem, rsem):
        def body(i, carry):
            peer = lax.rem(o + i, NO)
            pltpu.make_async_remote_copy(
                src_ref=src.at[c, pl.ds(pl.multiple_of(peer * 8, 8), 8), :],
                dst_ref=dst.at[c, pl.ds(pl.multiple_of(o * 8, 8), 8), :],
                send_sem=ssem.at[c],
                recv_sem=rsem.at[c],
                device_id=(peer, l),
                device_id_type=MESH,
            ).start()
            return carry

        lax.fori_loop(1, NO, body, 0)
        at = pl.ds(pl.multiple_of(o * 8, 8), 8)
        dst[c, at, :] = src[c, at, :]

    def take_all(ref, c, sem):
        part_ref = ref.at[c, pl.ds(0, 8 * (NO - 1)), :]
        pltpu.make_async_copy(part_ref, part_ref, sem.at[c]).wait()

    def synth_near(c):
        synth(c, l, True)
        ag(c, 2, left, HALF, right).wait_recv()
        synth(c, left, False)
        ag(c, 3, right, 0, left).wait_recv()
        synth(c, right, False)

    def synth_far(c):
        ag(c, 4, opp, 0, right).wait_recv()
        ag(c, 5, opp, HALF, left).wait_recv()
        synth(c, opp, False)
        sy[c] = wide_to_tall(rs_acc[...])
        all_to_all(sy, r, c, a2_s, a2_r)

    def reduce_start(i, value):
        v1[i, o] = value

        def body(k, carry):
            peer = lax.rem(o + k, NO)
            pltpu.make_async_remote_copy(
                src_ref=v1.at[i, o],
                dst_ref=v1.at[i, o],
                send_sem=v1_s.at[i],
                recv_sem=v1_r.at[i],
                device_id=(peer, l),
                device_id_type=MESH,
            ).start()
            return carry

        lax.fori_loop(1, NO, body, 0)

    def v2_copy(i, k):
        return pltpu.make_async_remote_copy(
            src_ref=v2.at[i, l],
            dst_ref=v2.at[i, l],
            send_sem=v2_s.at[i],
            recv_sem=v2_r.at[i],
            device_id=(o, lax.rem(l + k, NL)),
            device_id_type=MESH,
        )

    def reduce_middle(i):
        got = v1.at[i, pl.ds(0, NO - 1)]
        pltpu.make_async_copy(got, got, v1_r.at[i]).wait()
        v2[i, l] = jnp.sum(v1[i], axis=0)
        for k in range(1, NL):
            v2_copy(i, k).start()

    def reduce_end(i):
        got = v2.at[i, pl.ds(0, NL - 1)]
        pltpu.make_async_copy(got, got, v2_r.at[i]).wait()
        return jnp.sum(v2[i], axis=0)

    group = iota((64, 128), 1) >> 5

    def grid_stage(c):
        take_all(r, c, a2_r)
        parts = [[None] * 2 for _ in range(4)]
        for tt in range(8):
            x = r[c, pl.ds(tt, NO, stride=8), :]
            u = tt % 4
            for p in range(4):
                y = pltpu.roll(x, 32 * ((u - p) % 4), 1) if u != p else x
                old = parts[p][tt // 4]
                parts[p][tt // 4] = y if old is None else jnp.where(group == u, y, old)
        mat = jnp.concatenate([jnp.concatenate(parts[p], axis=1) for p in range(4)], axis=0)
        hi, lo = split(mat)
        surface = mm(hth[...], hi) + (mm(hth[...], lo) + mm(htl[...], hi))
        weighted = wx[...] * surface
        curve = jnp.sum(weighted * surface, axis=0, keepdims=True)
        curve = curve[:, 0:128] + curve[:, 128:256]
        hi, lo = split(weighted)
        spectra = mm(hh[...], hi) + (mm(hh[...], lo) + mm(hl[...], hi))
        for tt in range(8):
            u = tt % 4
            y = None
            for p in range(4):
                x = spectra[64 * p : 64 * p + 64, 128 * (tt // 4) : 128 * (tt // 4) + 128]
                if u != p:
                    x = pltpu.roll(x, 32 * ((p - u) % 4), 1)
                y = x if y is None else jnp.where(group == p, x, y)
            t[c, pl.ds(tt, NO, stride=8), :] = y
        all_to_all(t, q, c, b2_s, b2_r)
        reduce_start(c, jnp.concatenate([norm_before[c], curve + damped[c]], axis=0))

    low = iota((SLOT, 128), 1) < 64
    low_q = iota((BAND, 128), 1) < 64

    def analysis_operands(c):
        take_all(q, c, b2_r)
        x = q[c]
        hi, lo = split(x)
        hif = hi.astype(F32)
        lof = pltpu.roll(lo.astype(F32), 64, 1)
        zero = jnp.zeros_like(x)
        one = [jnp.where(low_q, hif, lof).astype(BF16), jnp.where(low_q, lof, hif).astype(BF16)]
        two = [jnp.where(low_q, hif, zero).astype(BF16), jnp.where(low_q, zero, hif).astype(BF16)]
        return one, two

    def analysis(c, slot, operands):
        one, two = operands
        p0 = mm(lh[0, slot], one[0])
        p1 = mm(lh[1, slot], one[1])
        tail = mm(ll[0, slot], two[0]) + mm(ll[1, slot], two[1])
        first = jnp.where(low, p0, p1)
        second = pltpu.roll(jnp.where(low, p1, p0), 64, 1)
        pp[c, slot] = first + second + tail

    def rs_one(c, k, lo, to):
        return pltpu.make_async_remote_copy(
            src_ref=pp.at[c, opp, pl.ds(lo, HALF), :],
            dst_ref=ra.at[c, k],
            send_sem=rs_s.at[c, k],
            recv_sem=rs_r.at[c, k],
            device_id=(o, to),
            device_id_type=MESH,
        )

    def rs_two(c, k, side, slot, lo, to):
        return pltpu.make_async_remote_copy(
            src_ref=pp.at[c, slot, pl.ds(lo, HALF), :],
            dst_ref=rb.at[c, side, pl.ds(lo, HALF), :],
            send_sem=rs_s.at[c, k],
            recv_sem=rs_r.at[c, k],
            device_id=(o, to),
            device_id_type=MESH,
        )

    def scatter_start(c):
        operands = analysis_operands(c)
        analysis(c, opp, operands)
        rs_one(c, 0, 0, right).start()
        rs_one(c, 1, HALF, left).start()
        analysis(c, right, operands)
        rs_two(c, 2, 0, right, HALF, right).start()
        analysis(c, left, operands)
        rs_two(c, 3, 1, left, 0, left).start()
        analysis(c, l, operands)

    def scatter_middle(c):
        rs_one(c, 0, 0, right).wait_recv()
        pp[c, right, 0:HALF, :] = pp[c, right, 0:HALF, :] + ra[c, 0]
        rs_two(c, 4, 0, right, 0, right).start()
        rs_one(c, 1, HALF, left).wait_recv()
        pp[c, left, HALF:SLOT, :] = pp[c, left, HALF:SLOT, :] + ra[c, 1]
        rs_two(c, 5, 1, left, HALF, left).start()

    def store(ref, c, value):
        for p in range(4):
            ref[p // 2, p % 2, c * KC : (c + 1) * KC, :] = value[32 * p : 32 * p + 32, 0:DEG]

    def scatter_end(c):
        sums = fold_sums(c)
        rs_two(c, 2, 0, right, HALF, right).wait_recv()
        rs_two(c, 3, 1, left, 0, left).wait_recv()
        rs_two(c, 4, 0, right, 0, right).wait_recv()
        rs_two(c, 5, 1, left, HALF, left).wait_recv()
        x = pp[c, l] + (rb[c, 0] + rb[c, 1])
        x = tall_to_wide(jnp.concatenate([x, jnp.zeros((WIDE - SLOT, 128), F32)], axis=0))
        x = jnp.where(odd == 1, pltpu.roll(x, WIDE - 4, 1), x)
        y = dn[c]
        applied = jnp.where(valid, x + dampp[...] * y, 0.0)
        step = jnp.concatenate([column(sums[0:1] / sums[1:2])] * (WIDE // 128), axis=1)
        new_res = nres_v[c] - step * applied
        nres_v[c] = new_res
        z = row_sum(new_res * new_res)
        reduce_start(CH + c, jnp.concatenate([z, z], axis=0))
        store(res_v, c, new_res)
        sy_pos = natural(pos_v, c)
        masked = jnp.where(valid[:, 0:DEG], sy_pos, 0.0)
        new_pos = masked + (step * y)[:, 0:DEG]
        store(pos_v, c, new_pos)

    def fold_sums(c):
        return fold4(reduce_end(c))

    def finish(c):
        after = fold4(reduce_end(CH + c))[0:1]
        before = fold4(jnp.sum(v2[c], axis=0))[0:1]
        ratio = jnp.concatenate([column(after / before)] * (WIDE // 128), axis=1)
        store(dir_v, c, nres_v[c] + ratio * dn[c])

    synth_near(0)
    synth_far(0)
    ag_forward(1)
    synth_near(1)
    grid_stage(0)
    synth_far(1)
    reduce_middle(0)
    scatter_start(0)
    grid_stage(1)
    scatter_middle(0)
    reduce_middle(1)
    scatter_start(1)
    in_pos.wait()
    scatter_end(0)
    scatter_middle(1)
    reduce_middle(CH)
    scatter_end(1)
    out_res = pltpu.make_async_copy(res_v, nres_h, osem.at[0])
    out_pos = pltpu.make_async_copy(pos_v, npos_h, osem.at[1])
    out_res.start()
    out_pos.start()
    finish(0)
    reduce_middle(CH + 1)
    finish(1)
    out_dir = pltpu.make_async_copy(dir_v, ndir_h, osem.at[2])
    out_dir.start()

    for c in range(CH):
        ag(c, 0, l, 0, right).wait_send()
        ag(c, 1, l, HALF, left).wait_send()
        ag(c, 2, l, HALF, right).wait_send()
        ag(c, 3, l, 0, left).wait_send()
        ag(c, 4, left, 0, right).wait_send()
        ag(c, 5, right, HALF, left).wait_send()
        rs_one(c, 0, 0, right).wait_send()
        rs_one(c, 1, HALF, left).wait_send()
        rs_two(c, 2, 0, right, HALF, right).wait_send()
        rs_two(c, 3, 1, left, 0, left).wait_send()
        rs_two(c, 4, 0, right, 0, right).wait_send()
        rs_two(c, 5, 1, left, HALF, left).wait_send()
        take_all(sy, c, a2_s)
        take_all(t, c, b2_s)
    for i in range(2 * CH):
        sent = v1.at[i, pl.ds(0, NO - 1)]
        pltpu.make_async_copy(sent, sent, v1_s.at[i]).wait()
        sent = v2.at[i, pl.ds(0, NL - 1)]
        pltpu.make_async_copy(sent, sent, v2_s.at[i]).wait()
    out_res.wait()
    out_pos.wait()
    out_dir.wait()


def shards(
    position, residual, direction, legendre, order_of, class_idx, land, class_weight, damping
):
    any_spec = pl.BlockSpec(memory_space=pl.ANY)
    smem = pl.BlockSpec(memory_space=pltpu.SMEM)
    vmem = pl.BlockSpec(memory_space=pltpu.VMEM)
    dma = pltpu.SemaphoreType.DMA
    block = (2, 2, 64, DEG)
    return pl.pallas_call(
        kernel,
        out_shape=[jax.ShapeDtypeStruct(block, F32)] * 3,
        in_specs=[any_spec] * 6 + [smem, vmem, smem, vmem],
        out_specs=[any_spec] * 3,
        scratch_shapes=[
            pltpu.VMEM((2, NL, SLOT, BAND), F32),
            pltpu.VMEM((2, NL, SLOT, BAND), BF16),
            pltpu.VMEM((2, NL, SLOT, BAND), BF16),
            pltpu.VMEM(block, F32),
            pltpu.VMEM(block, F32),
            pltpu.VMEM(block, F32),
            pltpu.VMEM((8, NLON), jnp.int32),
            pltpu.VMEM((8, NLON), jnp.int32),
            pltpu.VMEM((8, 4608), F32),
            pltpu.VMEM((CH, 128, WIDE), F32),
            pltpu.VMEM((1, WIDE), F32),
            pltpu.VMEM((CH, NL, SLOT, 128), F32),
            pltpu.VMEM((CH, BAND, 128), F32),
            pltpu.VMEM((CH, BAND, 128), F32),
            pltpu.VMEM((CH, BAND, 128), F32),
            pltpu.VMEM((CH, BAND, 128), F32),
            pltpu.VMEM((CH, NL, SLOT, 128), F32),
            pltpu.VMEM((CH, 2, HALF, 128), F32),
            pltpu.VMEM((CH, 2, SLOT, 128), F32),
            pltpu.VMEM((2 * CH, NO, 2, 128), F32),
            pltpu.VMEM((2 * CH, NL, 2, 128), F32),
            pltpu.VMEM((CH, 128, WIDE), F32),
            pltpu.VMEM((ROWS_J, 256), BF16),
            pltpu.VMEM((ROWS_J, 256), BF16),
            pltpu.VMEM((256, ROWS_J), BF16),
            pltpu.VMEM((256, ROWS_J), BF16),
            pltpu.VMEM((ROWS_J, 256), F32),
            pltpu.VMEM((128, BAND), F32),
            dma((8,)),
            dma((5,)),
            dma((3,)),
            dma((CH, 6)),
            dma((CH, 6)),
            dma((CH,)),
            dma((CH,)),
            dma((CH,)),
            dma((CH,)),
            dma((CH, 6)),
            dma((CH, 6)),
            dma((2 * CH,)),
            dma((2 * CH,)),
            dma((2 * CH,)),
            dma((2 * CH,)),
        ],
        compiler_params=pltpu.CompilerParams(
            collective_id=0, has_side_effects=True, vmem_limit_bytes=60 * 1024 * 1024
        ),
        name="cg_iteration",
    )(
        position, residual, direction, legendre, class_idx, land,
        order_of, order_of.reshape(1, -1), class_weight, damping.reshape(1, -1),
    )


def solution(mesh):
    return jax.shard_map(
        shards,
        mesh=mesh,
        in_specs=(
            P("order", None, None, "lat"),
            P("order", None, None, "lat"),
            P("order", None, None, "lat"),
            P("order", None, "lat"),
            P(),
            P(("lat", "order"), None),
            P(("lat", "order"), None),
            P(),
            P("lat"),
        ),
        out_specs=(
            P("order", None, None, "lat"),
            P("order", None, None, "lat"),
            P("order", None, None, "lat"),
        ),
        check_vma=False,
    )
```

time: 429 us -> 99.8 us (0.23); the launches traced: 420 us -> 99.5 us
  blocking collectives: 174 us -> 0 us
  waiting for transfers between devices: 123 us -> 0 us
  Pallas kernels: 0 us -> 90.3 us
  matrix products: 67.5 us -> 0 us
  other arithmetic: 21.7 us -> 0 us
  between operations: 14.7 us -> 0.64 us
  starting transfers between devices: 11.4 us -> 0 us
    psum x2 -> x0, blocking collectives: 150 us -> none  [the longest x1 76 us: shards(): norm_before = lax.psum(sample_sums(res_m * res_m), ('order', 'lat'))]
    pallas_call x0 -> x1, Pallas kernels: none -> 90.3 us  [shards(): pl.pallas_call(kernel, out_shape=[jax.ShapeDtypeStruct(block, F32)] * 3,...]
    dot_general x5 -> x0, matrix products: 67.5 us -> none  [the longest x1 31 us: shards(): surface = jnp.einsum('mrsk,sml->rkl', grid_in, harmonic, precision=highest)]
    psum x1 -> x0, waiting for transfers between devices: 61.3 us -> none  [shards(): totals = lax.psum(band_part, 'lat')]
    all_gather x1 -> x0, waiting for transfers between devices: 44.9 us -> none  [shards(): block_part = lax.all_gather(direction, 'lat', axis=3, tiled=True)]
    all_to_all x1 -> x0, blocking collectives: 23.4 us -> none  [shards(): lax.all_to_all(spectra.reshape(orders_all, rows_here, 2 * samples), 'orde...]
    all_to_all x1 -> x0, waiting for transfers between devices: 17.1 us -> none  [shards(): lax.all_to_all(synthesis.reshape(m_local, band_rows, 2 * samples), 'order...]
    all_to_all x1 -> x0, starting transfers between devices: 10.8 us -> none  [shards(): lax.all_to_all(synthesis.reshape(m_local, band_rows, 2 * samples), 'order...]
  transfers between devices with their start and end apart: 3 -> 0, of which waited for: 3 -> 0; matrix products, arithmetic and copies ran while one was open for 3% -> 0% of each run, Pallas kernels for 0% -> 0%
where the time goes in v1:
time: 99.8 us; the launch traced here: 99.5 us
  Pallas kernels  90.3 us (90%)
  local copies, waits for them, and re-layouts  8.53 us (9%)
    pallas_call x1, Pallas kernels, shards(): pl.pallas_call(kernel, out_shape=[jax.ShapeDtypeStruct(block, F32)] * 3,...  90.3 us
    unnamed x4, local copies, waits for them, and re-layouts  7.26 us

profile of v1, /device:TPU:1, one launch (start us, length us, event | category | flops | bytes accessed | tf_op | source)
XLA Modules:
  0.0 99.5 jit_solution(6711804915488063039)
XLA Ops:
  0.6 1.3 %reshape.13.damp_v = f32[1,540]{1,0:T(1,128)} reshape(f32[540]{0:T(1024)} %param.17) | data formatting | bytes 4320 | tf_op jit(solution)/shard_map/reshape | solution.py:577
  1.9 1.4 %copy.12.cw_s = f32[16,2]{1,0:T(8,128)} copy(f32[16,2]{0,1:T(2,128)} %param.16) | data formatting | bytes 256 | tf_op args[7]
  3.2 90.3 %cg_iteration.1 = (f32[2,2,64,540]{3,2,1,0:T(8,128)}, f32[2,2,64,540]{3,2,1,0:T(8,128)}, f32[2,2,64,540]{3,2,1,0:T(8,128)}) custom-call(f32[2,2,64,540]{3,2,1,0:T(8,128)} %pos_h.1, f32[2,2,64,540]{3,2,1,0:T(8,128)} %res_h.1, f32[2,2,64,540]{3,2,1,0:T(8,128)} %dir_h.1, f32[2,2160,512]{2,1,0:T(8,128)} %leg_h.1, s32[8,4320]{1,0:T(8,128)} %cls_h.1, ...), custom_call_target="tpu_custom_call" | custom-call | tf_op jit(solution)/shard_map/cg_iteration/pallas_call | solution.py:521
  93.6 2.0 %copy.16 = f32[2,2,64,540]{3,2,1,0:T(8,128)} copy(f32[2,2,64,540]{3,2,1,0:T(8,128)} %get-tuple-element.6) | data formatting | bytes 1105920
  95.5 2.0 %copy.17 = f32[2,2,64,540]{3,2,1,0:T(8,128)} copy(f32[2,2,64,540]{3,2,1,0:T(8,128)} %get-tuple-element.7) | data formatting | bytes 1105920
  97.5 2.0 %copy.18 = f32[2,2,64,540]{3,2,1,0:T(8,128)} copy(f32[2,2,64,540]{3,2,1,0:T(8,128)} %get-tuple-element.8) | data formatting | bytes 1105920

commit v2 on v1

--- a/solution.py
+++ b/solution.py
@@ -56,23 +56,16 @@
     return y + pltpu.roll(y, 32, 1)
 
 
-def row_sum(x):
-    acc = x[:, 0:128]
-    for i in range(1, WIDE // 128):
-        acc = acc + x[:, 128 * i : 128 * (i + 1)]
-    return jnp.sum(acc.T, axis=0, keepdims=True)
-
-
 def column(row):
     return jnp.broadcast_to(row, (128, 128)).T
 
 
 def kernel(
-    pos_h, res_h, dir_h, leg_h, cls_h, land_h, order_s, order_v, cw_s, damp_v,
-    npos_h, nres_h, ndir_h,
-    lf, lh, ll, dir_v, res_v, pos_v, cls_v, land_v, wv,
-    dn, dampp, g, sy, r, t, q, pp, ra, rb, v1, v2, nres_v,
-    hth, htl, hh, hl, wx, rs_acc,
+    res_h, dir_h, leg_h, cls_h, land_h, order_h, order_w, cw_h, damp_h,
+    app_h, cols_v, order_s, order_v, cw_s, damp_v,
+    lf, lh, ll, dir_v, res_v, app_v, cls_v, land_v, wv,
+    dn, dampp, g, sy, r, t, q, pp, ra, rb, v1, v2,
+    rt, dampt, validt, hth, htl, hh, hl, wx, rs_acc,
     lsem, isem, osem, ag_s, ag_r, a2_s, a2_r, b2_s, b2_r, rs_s, rs_r, v1_s, v1_r, v2_s, v2_r,
 ):
     o = lax.axis_index("order")
@@ -84,6 +77,28 @@
 
     in_dir = pltpu.make_async_copy(dir_h, dir_v, isem.at[0])
     in_dir.start()
+    in_order = pltpu.make_async_copy(order_h, order_s, isem.at[2])
+    in_order.start()
+    barrier = pltpu.get_barrier_semaphore()
+
+    def order_peer(i):
+        k = i >> 3
+        dz = 4 + ((k + 1) >> 1) * (1 - 2 * (k & 1))
+        j = (i & 7) + ((k + 1) >> 3)
+        return ((o + dz * 8) & 56) + ((o + j) & 7)
+
+    def greet(i, carry):
+        pl.semaphore_signal(
+            barrier, inc=1, device_id=(order_peer(i), l), device_id_type=MESH
+        )
+        return carry
+
+    for i in range(1, NL):
+        pl.semaphore_signal(
+            barrier, inc=1, device_id=(o, lax.rem(l + i, NL)), device_id_type=MESH
+        )
+    lax.fori_loop(0, NO - 1, greet, 0)
+
     leg_in = []
     for b in range(NL):
         for m in range(2):
@@ -93,24 +108,14 @@
             c.start()
             leg_in.append(c)
     in_res = pltpu.make_async_copy(res_h, res_v, isem.at[1])
-    in_pos = pltpu.make_async_copy(pos_h, pos_v, isem.at[2])
     in_cls = pltpu.make_async_copy(cls_h, cls_v, isem.at[3])
     in_land = pltpu.make_async_copy(land_h, land_v, isem.at[4])
-    for c in (in_res, in_pos, in_cls, in_land):
+    in_wide = pltpu.make_async_copy(order_w, order_v, isem.at[5])
+    in_cw = pltpu.make_async_copy(cw_h, cw_s, isem.at[6])
+    in_damp = pltpu.make_async_copy(damp_h, damp_v, isem.at[7])
+    for c in (in_wide, in_cw, in_damp, in_cls, in_land, in_res):
         c.start()
-
-    barrier = pltpu.get_barrier_semaphore()
-
-    def greet(i, carry):
-        peer = lax.rem(o + i, NO)
-        pl.semaphore_signal(barrier, inc=1, device_id=(peer, l), device_id_type=MESH)
-        return carry
-
-    for i in range(1, NL):
-        pl.semaphore_signal(
-            barrier, inc=1, device_id=(o, lax.rem(l + i, NL)), device_id_type=MESH
-        )
-    lax.fori_loop(1, NO, greet, 0)
+    in_order.wait()
 
     row = iota((128, WIDE), 0)
     lane = iota((128, WIDE), 1)
@@ -123,14 +128,14 @@
             axis=0,
         )
 
+    def rows_of(x):
+        return wide_to_tall(jnp.where(odd == 1, pltpu.roll(x, 4, 1), x))[0:SLOT]
+
     in_dir.wait()
     for c in range(CH):
         dn[c, :, 512:WIDE] = jnp.zeros((128, 128), F32)
         dn[c, :, 0:DEG] = natural(dir_v, c)
-        x = jnp.where(valid, dn[c], 0.0)
-        dn[c] = x
-        shifted = jnp.where(odd == 1, pltpu.roll(x, 4, 1), x)
-        g[c, l] = wide_to_tall(shifted)[0:SLOT]
+        g[c, l] = rows_of(jnp.where(valid, dn[c], 0.0))
 
     pl.semaphore_wait(barrier, NO - 1 + NL - 1)
 
@@ -181,6 +186,9 @@
         for m in range(2):
             convert(b, m)
 
+    in_wide.wait()
+    in_cw.wait()
+    in_damp.wait()
     col = iota((128, 256), 1)
     pick = (iota((128, 256), 0) == 2 * (col & 63) + (col >> 7)).astype(F32)
     sixteenth = jnp.broadcast_to(order_v[...].astype(F32) * (1.0 / 16.0), (8, 128))
@@ -208,7 +216,7 @@
         on_land = land_v[:, lo_lane : lo_lane + n] == 1
         w = jnp.zeros((8, n), F32)
         for k in range(16):
-            w = jnp.where(cls == k, jnp.where(on_land, cw_s[k, 1], cw_s[k, 0]), w)
+            w = jnp.where(cls == k, jnp.where(on_land, cw_s[1, k], cw_s[0, k]), w)
         wv[:, lo_lane : lo_lane + n] = w
     folded = jnp.zeros((8, 512), F32)
     for i in range(NLON // PERIOD):
@@ -226,19 +234,20 @@
     )[0:ROWS_J]
 
     dampp[:, 512:WIDE] = jnp.zeros((1, 128), F32)
-    dampp[:, 0:DEG] = damp_v[...]
+    dampp[:, 0:DEG] = damp_v[...].reshape(1, DEG)
+    dampt[...] = rows_of(jnp.broadcast_to(dampp[...], (128, WIDE)))
+    validt[...] = rows_of(valid.astype(F32))
 
     in_res.wait()
     norm_before = []
     damped = []
     for c in range(CH):
-        nres_v[c, :, 512:WIDE] = jnp.zeros((128, 128), F32)
-        nres_v[c, :, 0:DEG] = natural(res_v, c)
-        x = jnp.where(valid, nres_v[c], 0.0)
-        nres_v[c] = x
-        norm_before.append(row_sum(x * x))
-        y = dn[c]
-        damped.append(row_sum(y * (y * dampp[...])))
+        dn[c, :, 0:DEG] = natural(res_v, c)
+        x = rows_of(jnp.where(valid, dn[c], 0.0))
+        rt[c] = x
+        norm_before.append(jnp.sum(x * x, axis=0, keepdims=True))
+        y = g[c, l]
+        damped.append(jnp.sum(y * (y * dampt[...]), axis=0, keepdims=True))
 
     def synth(c, slot, first):
         x = jnp.concatenate([g[c, slot], jnp.zeros((WIDE - SLOT, 128), F32)], axis=0)
@@ -257,7 +266,7 @@
 
     def all_to_all(src, dst, c, ssem, rsem):
         def body(i, carry):
-            peer = lax.rem(o + i, NO)
+            peer = order_peer(i)
             pltpu.make_async_remote_copy(
                 src_ref=src.at[c, pl.ds(pl.multiple_of(peer * 8, 8), 8), :],
                 dst_ref=dst.at[c, pl.ds(pl.multiple_of(o * 8, 8), 8), :],
@@ -268,7 +277,7 @@
             ).start()
             return carry
 
-        lax.fori_loop(1, NO, body, 0)
+        lax.fori_loop(0, NO - 1, body, 0)
         at = pl.ds(pl.multiple_of(o * 8, 8), 8)
         dst[c, at, :] = src[c, at, :]
 
@@ -294,7 +303,7 @@
         v1[i, o] = value
 
         def body(k, carry):
-            peer = lax.rem(o + k, NO)
+            peer = order_peer(k)
             pltpu.make_async_remote_copy(
                 src_ref=v1.at[i, o],
                 dst_ref=v1.at[i, o],
@@ -305,7 +314,7 @@
             ).start()
             return carry
 
-        lax.fori_loop(1, NO, body, 0)
+        lax.fori_loop(0, NO - 1, body, 0)
 
     def v2_copy(i, k):
         return pltpu.make_async_remote_copy(
@@ -434,20 +443,16 @@
         rs_two(c, 4, 0, right, 0, right).wait_recv()
         rs_two(c, 5, 1, left, HALF, left).wait_recv()
         x = pp[c, l] + (rb[c, 0] + rb[c, 1])
-        x = tall_to_wide(jnp.concatenate([x, jnp.zeros((WIDE - SLOT, 128), F32)], axis=0))
+        step = sums[0:1] / sums[1:2]
+        applied = jnp.where(validt[...] > 0.5, x + dampt[...] * g[c, l], 0.0)
+        new_res = rt[c] - step * applied
+        z = jnp.sum(new_res * new_res, axis=0, keepdims=True)
+        reduce_start(CH + c, jnp.concatenate([z, z], axis=0))
+        x = jnp.concatenate([applied, jnp.zeros((WIDE - SLOT, 128), F32)], axis=0)
+        x = tall_to_wide(x)
         x = jnp.where(odd == 1, pltpu.roll(x, WIDE - 4, 1), x)
-        y = dn[c]
-        applied = jnp.where(valid, x + dampp[...] * y, 0.0)
-        step = jnp.concatenate([column(sums[0:1] / sums[1:2])] * (WIDE // 128), axis=1)
-        new_res = nres_v[c] - step * applied
-        nres_v[c] = new_res
-        z = row_sum(new_res * new_res)
-        reduce_start(CH + c, jnp.concatenate([z, z], axis=0))
-        store(res_v, c, new_res)
-        sy_pos = natural(pos_v, c)
-        masked = jnp.where(valid[:, 0:DEG], sy_pos, 0.0)
-        new_pos = masked + (step * y)[:, 0:DEG]
-        store(pos_v, c, new_pos)
+        store(app_v, c, x)
+        cols_v[0, c * KC : (c + 1) * KC, :] = column(step)[0:KC]
 
     def fold_sums(c):
         return fold4(reduce_end(c))
@@ -455,35 +460,29 @@
     def finish(c):
         after = fold4(reduce_end(CH + c))[0:1]
         before = fold4(jnp.sum(v2[c], axis=0))[0:1]
-        ratio = jnp.concatenate([column(after / before)] * (WIDE // 128), axis=1)
-        store(dir_v, c, nres_v[c] + ratio * dn[c])
+        cols_v[1, c * KC : (c + 1) * KC, :] = column(after / before)[0:KC]
 
     synth_near(0)
     synth_far(0)
     ag_forward(1)
     synth_near(1)
+    synth_far(1)
     grid_stage(0)
-    synth_far(1)
+    grid_stage(1)
+    scatter_start(0)
     reduce_middle(0)
-    scatter_start(0)
-    grid_stage(1)
     scatter_middle(0)
+    scatter_start(1)
     reduce_middle(1)
-    scatter_start(1)
-    in_pos.wait()
     scatter_end(0)
     scatter_middle(1)
     reduce_middle(CH)
     scatter_end(1)
-    out_res = pltpu.make_async_copy(res_v, nres_h, osem.at[0])
-    out_pos = pltpu.make_async_copy(pos_v, npos_h, osem.at[1])
-    out_res.start()
-    out_pos.start()
+    out_app = pltpu.make_async_copy(app_v, app_h, osem.at[0])
+    out_app.start()
     finish(0)
     reduce_middle(CH + 1)
     finish(1)
-    out_dir = pltpu.make_async_copy(dir_v, ndir_h, osem.at[2])
-    out_dir.start()
 
     for c in range(CH):
         ag(c, 0, l, 0, right).wait_send()
@@ -505,25 +504,51 @@
         pltpu.make_async_copy(sent, sent, v1_s.at[i]).wait()
         sent = v2.at[i, pl.ds(0, NL - 1)]
         pltpu.make_async_copy(sent, sent, v2_s.at[i]).wait()
-    out_res.wait()
-    out_pos.wait()
-    out_dir.wait()
+    out_app.wait()
+
+
+def combine(pos_v, res_v, dir_v, app_v, order_s, cols_v, npos_h, nres_h, ndir_h, y, osem):
+    o = lax.axis_index("order")
+    l = lax.axis_index("lat")
+    degree = iota((64, DEG), 1) + l * DEG
+    step = jnp.concatenate([cols_v[0]] * 5, axis=1)[:, 0:DEG]
+    ratio = jnp.concatenate([cols_v[1]] * 5, axis=1)[:, 0:DEG]
+    outs = []
+    for m in range(2):
+        valid = degree >= order_s[2 * o + m]
+        for s in range(2):
+            pos, res, way = (jnp.where(valid, x[m, s], 0.0) for x in (pos_v, res_v, dir_v))
+            new_res = res - step * app_v[m, s]
+            y[0, m, s] = pos + step * way
+            y[1, m, s] = new_res
+            y[2, m, s] = new_res + ratio * way
+            for k, ref in enumerate((npos_h, nres_h, ndir_h)):
+                c = pltpu.make_async_copy(y.at[k, m, s], ref.at[m, s], osem.at[k, m, s])
+                c.start()
+                outs.append(c)
+    for c in outs:
+        c.wait()
 
 
 def shards(
     position, residual, direction, legendre, order_of, class_idx, land, class_weight, damping
 ):
     any_spec = pl.BlockSpec(memory_space=pl.ANY)
+    hbm = pl.BlockSpec(memory_space=pltpu.HBM)
     smem = pl.BlockSpec(memory_space=pltpu.SMEM)
     vmem = pl.BlockSpec(memory_space=pltpu.VMEM)
     dma = pltpu.SemaphoreType.DMA
     block = (2, 2, 64, DEG)
-    return pl.pallas_call(
+    applied, columns = pl.pallas_call(
         kernel,
-        out_shape=[jax.ShapeDtypeStruct(block, F32)] * 3,
-        in_specs=[any_spec] * 6 + [smem, vmem, smem, vmem],
-        out_specs=[any_spec] * 3,
+        out_shape=[jax.ShapeDtypeStruct(block, F32), jax.ShapeDtypeStruct((2, 64, 128), F32)],
+        in_specs=[hbm] * 9,
+        out_specs=[any_spec, vmem],
         scratch_shapes=[
+            pltpu.SMEM((128,), jnp.int32),
+            pltpu.VMEM((1, 128), jnp.int32),
+            pltpu.SMEM((2, 16), F32),
+            pltpu.VMEM((DEG,), F32),
             pltpu.VMEM((2, NL, SLOT, BAND), F32),
             pltpu.VMEM((2, NL, SLOT, BAND), BF16),
             pltpu.VMEM((2, NL, SLOT, BAND), BF16),
@@ -545,7 +570,9 @@
             pltpu.VMEM((CH, 2, SLOT, 128), F32),
             pltpu.VMEM((2 * CH, NO, 2, 128), F32),
             pltpu.VMEM((2 * CH, NL, 2, 128), F32),
-            pltpu.VMEM((CH, 128, WIDE), F32),
+            pltpu.VMEM((CH, SLOT, 128), F32),
+            pltpu.VMEM((SLOT, 128), F32),
+            pltpu.VMEM((SLOT, 128), F32),
             pltpu.VMEM((ROWS_J, 256), BF16),
             pltpu.VMEM((ROWS_J, 256), BF16),
             pltpu.VMEM((256, ROWS_J), BF16),
@@ -553,7 +580,7 @@
             pltpu.VMEM((ROWS_J, 256), F32),
             pltpu.VMEM((128, BAND), F32),
             dma((8,)),
-            dma((5,)),
+            dma((8,)),
             dma((3,)),
             dma((CH, 6)),
             dma((CH, 6)),
@@ -569,13 +596,30 @@
             dma((2 * CH,)),
         ],
         compiler_params=pltpu.CompilerParams(
-            collective_id=0, has_side_effects=True, vmem_limit_bytes=60 * 1024 * 1024
+            collective_id=0, has_side_effects=True, vmem_limit_bytes=36 * 1024 * 1024
         ),
         name="cg_iteration",
     )(
-        position, residual, direction, legendre, class_idx, land,
-        order_of, order_of.reshape(1, -1), class_weight, damping.reshape(1, -1),
+        *(
+            pltpu.with_memory_space_constraint(a, pltpu.HBM)
+            for a in (
+                residual, direction, legendre, class_idx, land,
+                order_of, order_of.reshape(1, -1), class_weight.T, damping,
+            )
+        )
     )
+    return pl.pallas_call(
+        combine,
+        out_shape=[jax.ShapeDtypeStruct(block, F32)] * 3,
+        in_specs=[vmem] * 4 + [smem, vmem],
+        out_specs=[any_spec] * 3,
+        scratch_shapes=[
+            pltpu.VMEM((3,) + block, F32),
+            dma((3, 2, 2)),
+        ],
+        compiler_params=pltpu.CompilerParams(vmem_limit_bytes=16 * 1024 * 1024),
+        name="combine",
+    )(position, residual, direction, applied, order_of, columns)
 
 
 def solution(mesh):

time: 99.8 us -> 83.2 us (0.83)
  local copies, waits for them, and re-layouts: 8.53 us -> 0.02 us
  Pallas kernels: 90.3 us -> 82.2 us
    pallas_call x1 -> x2, Pallas kernels: 90.3 us -> 82.2 us  [the longest x1 80.3 us: shards(): pl.pallas_call(kernel, out_shape=[jax.ShapeDtypeStruct(block, F32), jax.S...]
    unnamed x4 -> x8, local copies, waits for them, and re-layouts: 7.26 us -> 0.02 us
    reshape x1 -> x0, local copies, waits for them, and re-layouts: 1.27 us -> none  [shards(): damping.reshape(1, -1)]
where the time goes in v2:
time: 83.2 us; the launch traced here: 83.1 us
  Pallas kernels  82.2 us (99%)
  between operations  0.87 us (1%)
    pallas_call x1, Pallas kernels, shards(): pl.pallas_call(kernel, out_shape=[jax.ShapeDtypeStruct(block, F32), jax.S...  80.3 us
    pallas_call x1, Pallas kernels, shards(): pl.pallas_call(combine, out_shape=[jax.ShapeDtypeStruct(block, F32)] * 3,...  1.97 us

profile of v2, /device:TPU:1, one launch (start us, length us, event | category | flops | bytes accessed | tf_op | source)
XLA Modules:
  0.0 83.1 jit_solution(10786116754781462453)
XLA Ops:
  0.6 0.0 copy-start.3
  0.6 0.0 copy-start.1
  0.7 0.0 copy-start
  0.7 0.0 copy-start.2
  0.7 80.3 %cg_iteration.1 = (f32[2,2,64,540]{3,2,1,0:T(8,128)S(1)}, f32[2,64,128]{2,1,0:T(8,128)S(1)}) custom-call(f32[2,2,64,540]{3,2,1,0:T(8,128)} %res_v.1, f32[2,2,64,540]{3,2,1,0:T(8,128)} %dir_v.1, f32[2,2160,512]{2,1,0:T(8,128)} %leg_h.1, s32[8,4320]{1,0:T(8,128)} %cls_h.1, s32[8,4320]{1,0:T(8,128)} %land_h.1, s32[128]{0:T(128)} %order_s.1, s32[1,128]{1,0:T(1,128)} %bitcast.2, ...), custom_call_target="tpu_custom_call" | custom-call | tf_op jit(solution)/shard_map/cg_iteration/pallas_call | solution.py:542
  80.9 0.0 copy-done.3
  80.9 0.0 copy-done.1
  81.0 0.0 copy-done
  81.0 0.0 copy-done.2
  81.0 2.0 %combine.1 = (f32[2,2,64,540]{3,2,1,0:T(8,128)}, f32[2,2,64,540]{3,2,1,0:T(8,128)}, f32[2,2,64,540]{3,2,1,0:T(8,128)}) custom-call(f32[2,2,64,540]{3,2,1,0:T(8,128)S(1)} %copy-done.2, f32[2,2,64,540]{3,2,1,0:T(8,128)S(1)} %copy-done, f32[2,2,64,540]{3,2,1,0:T(8,128)S(1)} %copy-done.1, f32[2,2,64,540]{3,2,1,0:T(8,128)S(1)} %get-tuple-element.5.app_v, ...), custom_call_target="tpu_custom_call" | custom-call | tf_op jit(solution)/shard_map/combine/pallas_call | solution.py:611
Async XLA Ops:
  0.6 80.3 %copy-start.3 = (s32[128]{0:T(128)S(1)}, s32[128]{0:T(128)}, u32[]{:S(2)}) copy-start(s32[128]{0:T(128)} %order_s.1) | copy-start | bytes 1540
  0.6 80.3 %copy-start.1 = (f32[2,2,64,540]{3,2,1,0:T(8,128)S(1)}, f32[2,2,64,540]{3,2,1,0:T(8,128)}, u32[]{:S(2)}) copy-start(f32[2,2,64,540]{3,2,1,0:T(8,128)} %dir_v.1) | copy-start | bytes 1658884
  0.7 80.3 %copy-start = (f32[2,2,64,540]{3,2,1,0:T(8,128)S(1)}, f32[2,2,64,540]{3,2,1,0:T(8,128)}, u32[]{:S(2)}) copy-start(f32[2,2,64,540]{3,2,1,0:T(8,128)} %res_v.1) | copy-start | bytes 1658884
  0.7 80.3 %copy-start.2 = (f32[2,2,64,540]{3,2,1,0:T(8,128)S(1)}, f32[2,2,64,540]{3,2,1,0:T(8,128)}, u32[]{:S(2)}) copy-start(f32[2,2,64,540]{3,2,1,0:T(8,128)} %pos_v.1) | copy-start | bytes 1658884

commit v3 on v2

--- a/solution.py
+++ b/solution.py
@@ -21,7 +21,10 @@
 STARTS = (0, 536, 1080, 1616)
 BAND = 512
 CH = 2
-KC = 32
+NS = 4
+KS = 16
+PACK = SLOT // 2
+QH = PACK // 2
 PERIOD = 270
 NLON = 4320
 ROWS_J = 272
@@ -51,9 +54,18 @@
     return lax.broadcasted_iota(jnp.int32, shape, axis)
 
 
-def fold4(x):
+def fold8(x):
     y = x + pltpu.roll(x, 64, 1)
-    return y + pltpu.roll(y, 32, 1)
+    y = y + pltpu.roll(y, 32, 1)
+    return y + pltpu.roll(y, 16, 1)
+
+
+def pack(x, h):
+    low = iota((PACK, 128), 1) < 64
+    top, bottom = x[0:PACK], x[PACK:SLOT]
+    if h == 0:
+        return jnp.where(low, top, pltpu.roll(bottom, 64, 1))
+    return jnp.where(low, pltpu.roll(top, 64, 1), bottom)
 
 
 def column(row):
@@ -64,7 +76,7 @@
     res_h, dir_h, leg_h, cls_h, land_h, order_h, order_w, cw_h, damp_h,
     app_h, cols_v, order_s, order_v, cw_s, damp_v,
     lf, lh, ll, dir_v, res_v, app_v, cls_v, land_v, wv,
-    dn, dampp, g, sy, r, t, q, pp, ra, rb, v1, v2,
+    dn, dampp, g, gp, xs, sy, r, t, q, pp, ra, rb, v1, v2,
     rt, dampt, validt, hth, htl, hh, hl, wx, rs_acc,
     lsem, isem, osem, ag_s, ag_r, a2_s, a2_r, b2_s, b2_r, rs_s, rs_r, v1_s, v1_r, v2_s, v2_r,
 ):
@@ -97,7 +109,7 @@
         pl.semaphore_signal(
             barrier, inc=1, device_id=(o, lax.rem(l + i, NL)), device_id_type=MESH
         )
-    lax.fori_loop(0, NO - 1, greet, 0)
+    lax.fori_loop(0, NO - 1, greet, 0, unroll=9)
 
     leg_in = []
     for b in range(NL):
@@ -119,12 +131,17 @@
 
     row = iota((128, WIDE), 0)
     lane = iota((128, WIDE), 1)
-    order_row = jnp.where(row < 64, order_s[2 * o], order_s[2 * o + 1])
+    order_row = jnp.where((row & 32) == 0, order_s[2 * o], order_s[2 * o + 1])
     valid = (lane < DEG) & (lane + l * DEG >= order_row)
 
     def natural(ref, c):
         return jnp.concatenate(
-            [ref[m, s, c * KC : (c + 1) * KC, :] for m in range(2) for s in range(2)],
+            [
+                ref[m, s, (2 * c + h) * KS : (2 * c + h + 1) * KS, :]
+                for h in range(2)
+                for m in range(2)
+                for s in range(2)
+            ],
             axis=0,
         )
 
@@ -175,14 +192,7 @@
 
         lax.fori_loop(0, SLOT // 32, body, 0)
 
-    for b in range(NL // 2):
-        for m in range(2):
-            convert(b, m)
-
-    ag_forward(0)
-    ag_first(1)
-
-    for b in range(NL // 2, NL):
+    for b in range(NL):
         for m in range(2):
             convert(b, m)
 
@@ -228,62 +238,72 @@
         folded = folded + v
     folded = jnp.where(iota((8, 512), 1) < PERIOD, folded, 0.0) * (2.0 / NLON)
     folded = jnp.concatenate([folded[:, 0:384], jnp.zeros((120, 384), F32)], axis=0)
-    spread = (iota((128, 256), 0) == (iota((128, 256), 1) >> 5)).astype(F32)
+    spread = (iota((128, 128), 0) == (iota((128, 128), 1) >> 4)).astype(F32)
     wx[...] = jnp.dot(
         wide_to_tall(folded), spread, precision=lax.Precision.HIGHEST, preferred_element_type=F32
     )[0:ROWS_J]
 
-    dampp[:, 512:WIDE] = jnp.zeros((1, 128), F32)
-    dampp[:, 0:DEG] = damp_v[...].reshape(1, DEG)
-    dampt[...] = rows_of(jnp.broadcast_to(dampp[...], (128, WIDE)))
-    validt[...] = rows_of(valid.astype(F32))
-
-    in_res.wait()
-    norm_before = []
+    ag_forward(0)
+    ag_first(1)
+
+    norms = []
     damped = []
-    for c in range(CH):
-        dn[c, :, 0:DEG] = natural(res_v, c)
-        x = rows_of(jnp.where(valid, dn[c], 0.0))
-        rt[c] = x
-        norm_before.append(jnp.sum(x * x, axis=0, keepdims=True))
-        y = g[c, l]
-        damped.append(jnp.sum(y * (y * dampt[...]), axis=0, keepdims=True))
+
+    def prepare():
+        dampp[:, 512:WIDE] = jnp.zeros((1, 128), F32)
+        dampp[:, 0:DEG] = damp_v[...].reshape(1, DEG)
+        x = rows_of(jnp.broadcast_to(dampp[...], (128, WIDE)))
+        dampt[...] = pack(x, 0)
+        validt[...] = pack(rows_of(valid.astype(F32)), 0)
+        in_res.wait()
+        for c in range(CH):
+            dn[c, :, 0:DEG] = natural(res_v, c)
+            x = rows_of(jnp.where(valid, dn[c], 0.0))
+            y = g[c, l]
+            for h in range(2):
+                xh, yh = pack(x, h), pack(y, h)
+                rt[2 * c + h] = xh
+                gp[2 * c + h] = yh
+                norms.append(jnp.sum(xh * xh, axis=0, keepdims=True))
+                damped.append(jnp.sum(yh * (yh * dampt[...]), axis=0, keepdims=True))
 
     def synth(c, slot, first):
         x = jnp.concatenate([g[c, slot], jnp.zeros((WIDE - SLOT, 128), F32)], axis=0)
         wide = tall_to_wide(x)[:, 0:SLOT]
         hi, lo = split(wide)
         for m in range(2):
-            a = 64 * m
-            both = mm(
-                jnp.concatenate([hi[a : a + 64], lo[a : a + 64]], axis=0), lh[m, slot]
-            )
-            out = both[0:64] + both[64:128] + mm(hi[a : a + 64], ll[m, slot])
-            if first:
-                rs_acc[a : a + 64, :] = out
-            else:
-                rs_acc[a : a + 64, :] = rs_acc[a : a + 64, :] + out
-
-    def all_to_all(src, dst, c, ssem, rsem):
-        def body(i, carry):
-            peer = order_peer(i)
+            a = 32 * m
+            hi_m = jnp.concatenate([hi[a : a + 32], hi[a + 64 : a + 96]], axis=0)
+            lo_m = jnp.concatenate([lo[a : a + 32], lo[a + 64 : a + 96]], axis=0)
+            both = mm(jnp.concatenate([hi_m, lo_m], axis=0), lh[m, slot])
+            out = both[0:64] + both[64:128] + mm(hi_m, ll[m, slot])
+            for h in range(2):
+                at = slice(a + 64 * h, a + 64 * h + 32)
+                part = out[32 * h : 32 * h + 32]
+                rs_acc[at, :] = part if first else rs_acc[at, :] + part
+
+    def all_to_all(src, dst, i, ssem, rsem):
+        def body(k, carry):
+            peer = order_peer(k)
             pltpu.make_async_remote_copy(
-                src_ref=src.at[c, pl.ds(pl.multiple_of(peer * 8, 8), 8), :],
-                dst_ref=dst.at[c, pl.ds(pl.multiple_of(o * 8, 8), 8), :],
-                send_sem=ssem.at[c],
-                recv_sem=rsem.at[c],
+                src_ref=src.at[i, peer],
+                dst_ref=dst.at[i, o],
+                send_sem=ssem.at[i],
+                recv_sem=rsem.at[i],
                 device_id=(peer, l),
                 device_id_type=MESH,
             ).start()
             return carry
 
-        lax.fori_loop(0, NO - 1, body, 0)
-        at = pl.ds(pl.multiple_of(o * 8, 8), 8)
-        dst[c, at, :] = src[c, at, :]
-
-    def take_all(ref, c, sem):
-        part_ref = ref.at[c, pl.ds(0, 8 * (NO - 1)), :]
-        pltpu.make_async_copy(part_ref, part_ref, sem.at[c]).wait()
+        lax.fori_loop(0, NO - 1, body, 0, unroll=9)
+        dst[i, o] = src[i, o]
+
+    def take_all(ref, i, sem):
+        part_ref = ref.at[i, pl.ds(0, NO - 1)]
+        pltpu.make_async_copy(part_ref, part_ref, sem.at[i]).wait()
+
+    low_o = iota((NO, 128), 1) < 64
+    group = (iota((NO, 128), 1) >> 4) & 3
 
     def synth_near(c):
         synth(c, l, True)
@@ -296,8 +316,15 @@
         ag(c, 4, opp, 0, right).wait_recv()
         ag(c, 5, opp, HALF, left).wait_recv()
         synth(c, opp, False)
-        sy[c] = wide_to_tall(rs_acc[...])
-        all_to_all(sy, r, c, a2_s, a2_r)
+        xs[...] = wide_to_tall(rs_acc[...])
+        for rr in range(4):
+            x = xs[pl.ds(rr, NO, stride=8), :]
+            y = xs[pl.ds(rr + 4, NO, stride=8), :]
+            sy[2 * c, :, rr, :] = jnp.where(low_o, x, pltpu.roll(y, 64, 1))
+            sy[2 * c + 1, :, rr, :] = jnp.where(low_o, pltpu.roll(x, 64, 1), y)
+
+    def exchange(i):
+        all_to_all(sy, r, i, a2_s, a2_r)
 
     def reduce_start(i, value):
         v1[i, o] = value
@@ -314,7 +341,7 @@
             ).start()
             return carry
 
-        lax.fori_loop(0, NO - 1, body, 0)
+        lax.fori_loop(0, NO - 1, body, 0, unroll=9)
 
     def v2_copy(i, k):
         return pltpu.make_async_remote_copy(
@@ -338,64 +365,76 @@
         pltpu.make_async_copy(got, got, v2_r.at[i]).wait()
         return jnp.sum(v2[i], axis=0)
 
-    group = iota((64, 128), 1) >> 5
-
-    def grid_stage(c):
-        take_all(r, c, a2_r)
-        parts = [[None] * 2 for _ in range(4)]
-        for tt in range(8):
-            x = r[c, pl.ds(tt, NO, stride=8), :]
-            u = tt % 4
+    curves = [None] * NS
+
+    def grid_stage(i):
+        take_all(r, i, a2_r)
+        parts = [None] * 4
+        for rr in range(4):
+            x = r[i, :, rr, :]
             for p in range(4):
-                y = pltpu.roll(x, 32 * ((u - p) % 4), 1) if u != p else x
-                old = parts[p][tt // 4]
-                parts[p][tt // 4] = y if old is None else jnp.where(group == u, y, old)
-        mat = jnp.concatenate([jnp.concatenate(parts[p], axis=1) for p in range(4)], axis=0)
-        hi, lo = split(mat)
-        surface = mm(hth[...], hi) + (mm(hth[...], lo) + mm(htl[...], hi))
+                y = pltpu.roll(x, 16 * (rr - p) % 128, 1) if rr != p else x
+                parts[p] = y if rr == 0 else jnp.where(group == rr, y, parts[p])
+        hi, lo = split(jnp.concatenate(parts, axis=0))
+        both = mm(hth[...], jnp.concatenate([hi, lo], axis=1))
+        surface = both[:, 0:128] + (both[:, 128:256] + mm(htl[...], hi))
         weighted = wx[...] * surface
-        curve = jnp.sum(weighted * surface, axis=0, keepdims=True)
-        curve = curve[:, 0:128] + curve[:, 128:256]
+        curves[i] = jnp.sum(weighted * surface, axis=0, keepdims=True)
         hi, lo = split(weighted)
-        spectra = mm(hh[...], hi) + (mm(hh[...], lo) + mm(hl[...], hi))
-        for tt in range(8):
-            u = tt % 4
+        both = mm(hh[...], jnp.concatenate([hi, lo], axis=1))
+        spectra = both[:, 0:128] + (both[:, 128:256] + mm(hl[...], hi))
+        for rr in range(4):
             y = None
             for p in range(4):
-                x = spectra[64 * p : 64 * p + 64, 128 * (tt // 4) : 128 * (tt // 4) + 128]
-                if u != p:
-                    x = pltpu.roll(x, 32 * ((p - u) % 4), 1)
+                x = spectra[64 * p : 64 * p + 64]
+                if rr != p:
+                    x = pltpu.roll(x, 16 * (p - rr) % 128, 1)
                 y = x if y is None else jnp.where(group == p, x, y)
-            t[c, pl.ds(tt, NO, stride=8), :] = y
-        all_to_all(t, q, c, b2_s, b2_r)
-        reduce_start(c, jnp.concatenate([norm_before[c], curve + damped[c]], axis=0))
-
-    low = iota((SLOT, 128), 1) < 64
-    low_q = iota((BAND, 128), 1) < 64
-
-    def analysis_operands(c):
-        take_all(q, c, b2_r)
-        x = q[c]
-        hi, lo = split(x)
+            t[i, :, rr, :] = y
+        all_to_all(t, q, i, b2_s, b2_r)
+
+    octant = iota((1, 128), 1) >> 4
+
+    def join(rows):
+        x = jnp.zeros((1, 128), F32)
+        for k, y in enumerate(rows):
+            x = jnp.where(octant == k, fold8(y), x)
+        return x
+
+    def part_of(x, k):
+        return fold8(jnp.where(octant == k, x, 0.0))
+
+    def sums_start():
+        reduce_start(0, join(norms + [curves[i] + damped[i] for i in range(NS)]))
+
+    low = iota((PACK, 128), 1) < 64
+    low_t = iota((BAND, 128), 1) < 64
+    first_m = (iota((SLOT, 128), 1) & 32) == 0
+
+    def analysis_operands(i):
+        take_all(q, i, b2_r)
+        for rr in range(4):
+            x = q[i, :, rr, :]
+            xs[pl.ds(rr, NO, stride=8), :] = x
+            xs[pl.ds(rr + 4, NO, stride=8), :] = pltpu.roll(x, 64, 1)
+        hi, lo = split(xs[...])
         hif = hi.astype(F32)
         lof = pltpu.roll(lo.astype(F32), 64, 1)
-        zero = jnp.zeros_like(x)
-        one = [jnp.where(low_q, hif, lof).astype(BF16), jnp.where(low_q, lof, hif).astype(BF16)]
-        two = [jnp.where(low_q, hif, zero).astype(BF16), jnp.where(low_q, zero, hif).astype(BF16)]
+        one = jnp.where(low_t, hif, lof).astype(BF16)
+        two = jnp.where(low_t, hif, 0.0).astype(BF16)
         return one, two
 
-    def analysis(c, slot, operands):
+    def analysis(i, slot, operands):
         one, two = operands
-        p0 = mm(lh[0, slot], one[0])
-        p1 = mm(lh[1, slot], one[1])
-        tail = mm(ll[0, slot], two[0]) + mm(ll[1, slot], two[1])
-        first = jnp.where(low, p0, p1)
-        second = pltpu.roll(jnp.where(low, p1, p0), 64, 1)
-        pp[c, slot] = first + second + tail
+        p0, p1 = mm(lh[0, slot], one), mm(lh[1, slot], one)
+        t0, t1 = mm(ll[0, slot], two), mm(ll[1, slot], two)
+        x = jnp.where(first_m, p0, p1) + jnp.where(first_m, t0, t1)
+        x = x + pltpu.roll(x, 64, 1)
+        pp[i, slot] = jnp.where(low, x[0:PACK], x[PACK:SLOT])
 
     def rs_one(c, k, lo, to):
         return pltpu.make_async_remote_copy(
-            src_ref=pp.at[c, opp, pl.ds(lo, HALF), :],
+            src_ref=pp.at[c, opp, pl.ds(lo, QH), :],
             dst_ref=ra.at[c, k],
             send_sem=rs_s.at[c, k],
             recv_sem=rs_r.at[c, k],
@@ -405,8 +444,8 @@
 
     def rs_two(c, k, side, slot, lo, to):
         return pltpu.make_async_remote_copy(
-            src_ref=pp.at[c, slot, pl.ds(lo, HALF), :],
-            dst_ref=rb.at[c, side, pl.ds(lo, HALF), :],
+            src_ref=pp.at[c, slot, pl.ds(lo, QH), :],
+            dst_ref=rb.at[c, side, pl.ds(lo, QH), :],
             send_sem=rs_s.at[c, k],
             recv_sem=rs_r.at[c, k],
             device_id=(o, to),
@@ -417,89 +456,122 @@
         operands = analysis_operands(c)
         analysis(c, opp, operands)
         rs_one(c, 0, 0, right).start()
-        rs_one(c, 1, HALF, left).start()
+        rs_one(c, 1, QH, left).start()
         analysis(c, right, operands)
-        rs_two(c, 2, 0, right, HALF, right).start()
+        rs_two(c, 2, 0, right, QH, right).start()
         analysis(c, left, operands)
         rs_two(c, 3, 1, left, 0, left).start()
         analysis(c, l, operands)
 
     def scatter_middle(c):
         rs_one(c, 0, 0, right).wait_recv()
-        pp[c, right, 0:HALF, :] = pp[c, right, 0:HALF, :] + ra[c, 0]
+        pp[c, right, 0:QH, :] = pp[c, right, 0:QH, :] + ra[c, 0]
         rs_two(c, 4, 0, right, 0, right).start()
-        rs_one(c, 1, HALF, left).wait_recv()
-        pp[c, left, HALF:SLOT, :] = pp[c, left, HALF:SLOT, :] + ra[c, 1]
-        rs_two(c, 5, 1, left, HALF, left).start()
-
-    def store(ref, c, value):
+        rs_one(c, 1, QH, left).wait_recv()
+        pp[c, left, QH:PACK, :] = pp[c, left, QH:PACK, :] + ra[c, 1]
+        rs_two(c, 5, 1, left, QH, left).start()
+
+    def scatter_end(i):
+        before, curve = sums[i]
+        rs_two(i, 2, 0, right, QH, right).wait_recv()
+        rs_two(i, 3, 1, left, 0, left).wait_recv()
+        rs_two(i, 4, 0, right, 0, right).wait_recv()
+        rs_two(i, 5, 1, left, QH, left).wait_recv()
+        x = pp[i, l] + (rb[i, 0] + rb[i, 1])
+        step = before / curve
+        applied = jnp.where(validt[...] > 0.5, x + dampt[...] * gp[i], 0.0)
+        new_res = rt[i] - step * applied
+        after[i] = jnp.sum(new_res * new_res, axis=0, keepdims=True)
+        return step, applied
+
+    def scatter_out(i, step, applied):
+        x = jnp.concatenate([applied, jnp.zeros((384 - PACK, 128), F32)], axis=0)
+        x = tall_to_wide(x)
+        zero = jnp.zeros((64, WIDE - 384), F32)
+        x = jnp.concatenate([x[0:64], zero], axis=1) + pltpu.roll(
+            jnp.concatenate([x[64:128], zero], axis=1), PACK, 1
+        )
+        x = jnp.where(odd == 1, pltpu.roll(x, WIDE - 4, 1), x)
         for p in range(4):
-            ref[p // 2, p % 2, c * KC : (c + 1) * KC, :] = value[32 * p : 32 * p + 32, 0:DEG]
-
-    def scatter_end(c):
-        sums = fold_sums(c)
-        rs_two(c, 2, 0, right, HALF, right).wait_recv()
-        rs_two(c, 3, 1, left, 0, left).wait_recv()
-        rs_two(c, 4, 0, right, 0, right).wait_recv()
-        rs_two(c, 5, 1, left, HALF, left).wait_recv()
-        x = pp[c, l] + (rb[c, 0] + rb[c, 1])
-        step = sums[0:1] / sums[1:2]
-        applied = jnp.where(validt[...] > 0.5, x + dampt[...] * g[c, l], 0.0)
-        new_res = rt[c] - step * applied
-        z = jnp.sum(new_res * new_res, axis=0, keepdims=True)
-        reduce_start(CH + c, jnp.concatenate([z, z], axis=0))
-        x = jnp.concatenate([applied, jnp.zeros((WIDE - SLOT, 128), F32)], axis=0)
-        x = tall_to_wide(x)
-        x = jnp.where(odd == 1, pltpu.roll(x, WIDE - 4, 1), x)
-        store(app_v, c, x)
-        cols_v[0, c * KC : (c + 1) * KC, :] = column(step)[0:KC]
-
-    def fold_sums(c):
-        return fold4(reduce_end(c))
-
-    def finish(c):
-        after = fold4(reduce_end(CH + c))[0:1]
-        before = fold4(jnp.sum(v2[c], axis=0))[0:1]
-        cols_v[1, c * KC : (c + 1) * KC, :] = column(after / before)[0:KC]
-
+            app_v[p // 2, p % 2, i * KS : (i + 1) * KS, :] = x[16 * p : 16 * p + 16, 0:DEG]
+        cols_v[0, i * KS : (i + 1) * KS, :] = column(step)[0:KS]
+
+    sums = [None] * NS
+    after = [None] * NS
+
+    def sums_end():
+        got = reduce_end(0)
+        for i in range(NS):
+            sums[i] = (part_of(got, i), part_of(got, NS + i))
+
+    def norm_start():
+        reduce_start(1, join(after))
+
+    def finish():
+        got = reduce_end(1)
+        for i in range(NS):
+            ratio = column(part_of(got, i) / sums[i][0])
+            cols_v[1, i * KS : (i + 1) * KS, :] = ratio[0:KS]
+
+    def drain():
+        for c in range(CH):
+            ag(c, 0, l, 0, right).wait_send()
+            ag(c, 1, l, HALF, left).wait_send()
+            ag(c, 2, l, HALF, right).wait_send()
+            ag(c, 3, l, 0, left).wait_send()
+            ag(c, 4, left, 0, right).wait_send()
+            ag(c, 5, right, HALF, left).wait_send()
+        for i in range(NS):
+            rs_one(i, 0, 0, right).wait_send()
+            rs_one(i, 1, QH, left).wait_send()
+            rs_two(i, 2, 0, right, QH, right).wait_send()
+            rs_two(i, 3, 1, left, 0, left).wait_send()
+            rs_two(i, 4, 0, right, 0, right).wait_send()
+            rs_two(i, 5, 1, left, QH, left).wait_send()
+            take_all(sy, i, a2_s)
+            take_all(t, i, b2_s)
+
+    prepare()
     synth_near(0)
     synth_far(0)
+    exchange(0)
+    exchange(1)
     ag_forward(1)
     synth_near(1)
+    grid_stage(0)
     synth_far(1)
-    grid_stage(0)
+    exchange(2)
     grid_stage(1)
+    exchange(3)
     scatter_start(0)
-    reduce_middle(0)
+    grid_stage(2)
     scatter_middle(0)
     scatter_start(1)
-    reduce_middle(1)
-    scatter_end(0)
+    grid_stage(3)
+    sums_start()
     scatter_middle(1)
-    reduce_middle(CH)
-    scatter_end(1)
+    scatter_start(2)
+    scatter_start(3)
+    scatter_middle(2)
+    reduce_middle(0)
+    sums_end()
+    out0 = scatter_end(0)
+    out1 = scatter_end(1)
+    scatter_middle(3)
+    out2 = scatter_end(2)
+    out3 = scatter_end(3)
+    norm_start()
+    scatter_out(0, *out0)
+    scatter_out(1, *out1)
+    scatter_out(2, *out2)
+    scatter_out(3, *out3)
     out_app = pltpu.make_async_copy(app_v, app_h, osem.at[0])
     out_app.start()
-    finish(0)
-    reduce_middle(CH + 1)
-    finish(1)
-
-    for c in range(CH):
-        ag(c, 0, l, 0, right).wait_send()
-        ag(c, 1, l, HALF, left).wait_send()
-        ag(c, 2, l, HALF, right).wait_send()
-        ag(c, 3, l, 0, left).wait_send()
-        ag(c, 4, left, 0, right).wait_send()
-        ag(c, 5, right, HALF, left).wait_send()
-        rs_one(c, 0, 0, right).wait_send()
-        rs_one(c, 1, HALF, left).wait_send()
-        rs_two(c, 2, 0, right, HALF, right).wait_send()
-        rs_two(c, 3, 1, left, 0, left).wait_send()
-        rs_two(c, 4, 0, right, 0, right).wait_send()
-        rs_two(c, 5, 1, left, HALF, left).wait_send()
-        take_all(sy, c, a2_s)
-        take_all(t, c, b2_s)
-    for i in range(2 * CH):
+    drain()
+    reduce_middle(1)
+    finish()
+
+    for i in range(2):
         sent = v1.at[i, pl.ds(0, NO - 1)]
         pltpu.make_async_copy(sent, sent, v1_s.at[i]).wait()
         sent = v2.at[i, pl.ds(0, NL - 1)]
@@ -561,39 +633,41 @@
             pltpu.VMEM((CH, 128, WIDE), F32),
             pltpu.VMEM((1, WIDE), F32),
             pltpu.VMEM((CH, NL, SLOT, 128), F32),
-            pltpu.VMEM((CH, BAND, 128), F32),
-            pltpu.VMEM((CH, BAND, 128), F32),
-            pltpu.VMEM((CH, BAND, 128), F32),
-            pltpu.VMEM((CH, BAND, 128), F32),
-            pltpu.VMEM((CH, NL, SLOT, 128), F32),
-            pltpu.VMEM((CH, 2, HALF, 128), F32),
-            pltpu.VMEM((CH, 2, SLOT, 128), F32),
-            pltpu.VMEM((2 * CH, NO, 2, 128), F32),
-            pltpu.VMEM((2 * CH, NL, 2, 128), F32),
-            pltpu.VMEM((CH, SLOT, 128), F32),
-            pltpu.VMEM((SLOT, 128), F32),
-            pltpu.VMEM((SLOT, 128), F32),
+            pltpu.VMEM((NS, PACK, 128), F32),
+            pltpu.VMEM((BAND, 128), F32),
+            pltpu.VMEM((NS, NO, 4, 128), F32),
+            pltpu.VMEM((NS, NO, 4, 128), F32),
+            pltpu.VMEM((NS, NO, 4, 128), F32),
+            pltpu.VMEM((NS, NO, 4, 128), F32),
+            pltpu.VMEM((NS, NL, PACK, 128), F32),
+            pltpu.VMEM((NS, 2, QH, 128), F32),
+            pltpu.VMEM((NS, 2, PACK, 128), F32),
+            pltpu.VMEM((2, NO, 1, 128), F32),
+            pltpu.VMEM((2, NL, 1, 128), F32),
+            pltpu.VMEM((NS, PACK, 128), F32),
+            pltpu.VMEM((PACK, 128), F32),
+            pltpu.VMEM((PACK, 128), F32),
             pltpu.VMEM((ROWS_J, 256), BF16),
             pltpu.VMEM((ROWS_J, 256), BF16),
             pltpu.VMEM((256, ROWS_J), BF16),
             pltpu.VMEM((256, ROWS_J), BF16),
-            pltpu.VMEM((ROWS_J, 256), F32),
+            pltpu.VMEM((ROWS_J, 128), F32),
             pltpu.VMEM((128, BAND), F32),
             dma((8,)),
             dma((8,)),
             dma((3,)),
             dma((CH, 6)),
             dma((CH, 6)),
-            dma((CH,)),
-            dma((CH,)),
-            dma((CH,)),
-            dma((CH,)),
-            dma((CH, 6)),
-            dma((CH, 6)),
-            dma((2 * CH,)),
-            dma((2 * CH,)),
-            dma((2 * CH,)),
-            dma((2 * CH,)),
+            dma((NS,)),
+            dma((NS,)),
+            dma((NS,)),
+            dma((NS,)),
+            dma((NS, 6)),
+            dma((NS, 6)),
+            dma((2,)),
+            dma((2,)),
+            dma((2,)),
+            dma((2,)),
         ],
         compiler_params=pltpu.CompilerParams(
             collective_id=0, has_side_effects=True, vmem_limit_bytes=36 * 1024 * 1024

time: 83.2 us -> 82.4 us (level)
    pallas_call x1, Pallas kernels: 80.3 us -> 79.4 us  [shards(): pl.pallas_call(kernel, out_shape=[jax.ShapeDtypeStruct(block, F32), jax.S...]
where the time goes in v3:
time: 82.4 us; the launch traced here: 82.3 us
  Pallas kernels  81.4 us (99%)
  between operations  0.89 us (1%)
    pallas_call x1, Pallas kernels, shards(): pl.pallas_call(kernel, out_shape=[jax.ShapeDtypeStruct(block, F32), jax.S...  79.4 us
    pallas_call x1, Pallas kernels, shards(): pl.pallas_call(combine, out_shape=[jax.ShapeDtypeStruct(block, F32)] * 3,...  1.97 us

profile of v3, /device:TPU:1, one launch (start us, length us, event | category | flops | bytes accessed | tf_op | source)
XLA Modules:
  0.0 82.3 jit_solution(5723553932390137413)
XLA Ops:
  0.6 0.0 copy-start.3
  0.6 0.0 copy-start.1
  0.7 0.0 copy-start
  0.7 0.0 copy-start.2
  0.7 79.4 %cg_iteration.1 = (f32[2,2,64,540]{3,2,1,0:T(8,128)S(1)}, f32[2,64,128]{2,1,0:T(8,128)S(1)}) custom-call(f32[2,2,64,540]{3,2,1,0:T(8,128)} %res_v.1, f32[2,2,64,540]{3,2,1,0:T(8,128)} %dir_v.1, f32[2,2160,512]{2,1,0:T(8,128)} %leg_h.1, s32[8,4320]{1,0:T(8,128)} %cls_h.1, s32[8,4320]{1,0:T(8,128)} %land_h.1, s32[128]{0:T(128)} %order_s.1, s32[1,128]{1,0:T(1,128)} %bitcast.2, ...), custom_call_target="tpu_custom_call" | custom-call | tf_op jit(solution)/shard_map/cg_iteration/pallas_call | solution.py:614
  80.1 0.0 copy-done.3
  80.1 0.0 copy-done.1
  80.1 0.0 copy-done
  80.1 0.0 copy-done.2
  80.1 2.0 %combine.1 = (f32[2,2,64,540]{3,2,1,0:T(8,128)}, f32[2,2,64,540]{3,2,1,0:T(8,128)}, f32[2,2,64,540]{3,2,1,0:T(8,128)}) custom-call(f32[2,2,64,540]{3,2,1,0:T(8,128)S(1)} %copy-done.2, f32[2,2,64,540]{3,2,1,0:T(8,128)S(1)} %copy-done, f32[2,2,64,540]{3,2,1,0:T(8,128)S(1)} %copy-done.1, f32[2,2,64,540]{3,2,1,0:T(8,128)S(1)} %get-tuple-element.5.app_v, ...), custom_call_target="tpu_custom_call" | custom-call | tf_op jit(solution)/shard_map/combine/pallas_call | solution.py:685
Async XLA Ops:
  0.6 79.5 %copy-start.3 = (s32[128]{0:T(128)S(1)}, s32[128]{0:T(128)}, u32[]{:S(2)}) copy-start(s32[128]{0:T(128)} %order_s.1) | copy-start | bytes 1540
  0.6 79.5 %copy-start.1 = (f32[2,2,64,540]{3,2,1,0:T(8,128)S(1)}, f32[2,2,64,540]{3,2,1,0:T(8,128)}, u32[]{:S(2)}) copy-start(f32[2,2,64,540]{3,2,1,0:T(8,128)} %dir_v.1) | copy-start | bytes 1658884
  0.7 79.5 %copy-start = (f32[2,2,64,540]{3,2,1,0:T(8,128)S(1)}, f32[2,2,64,540]{3,2,1,0:T(8,128)}, u32[]{:S(2)}) copy-start(f32[2,2,64,540]{3,2,1,0:T(8,128)} %res_v.1) | copy-start | bytes 1658884
  0.7 79.5 %copy-start.2 = (f32[2,2,64,540]{3,2,1,0:T(8,128)S(1)}, f32[2,2,64,540]{3,2,1,0:T(8,128)}, u32[]{:S(2)}) copy-start(f32[2,2,64,540]{3,2,1,0:T(8,128)} %pos_v.1) | copy-start | bytes 1658884

commit v4 on v3

--- a/solution.py
+++ b/solution.py
@@ -322,9 +322,8 @@
             y = xs[pl.ds(rr + 4, NO, stride=8), :]
             sy[2 * c, :, rr, :] = jnp.where(low_o, x, pltpu.roll(y, 64, 1))
             sy[2 * c + 1, :, rr, :] = jnp.where(low_o, pltpu.roll(x, 64, 1), y)
-
-    def exchange(i):
-        all_to_all(sy, r, i, a2_s, a2_r)
+        for h in range(2):
+            all_to_all(sy, r, 2 * c + h, a2_s, a2_r)
 
     def reduce_start(i, value):
         v1[i, o] = value
@@ -513,47 +512,25 @@
             ratio = column(part_of(got, i) / sums[i][0])
             cols_v[1, i * KS : (i + 1) * KS, :] = ratio[0:KS]
 
-    def drain():
-        for c in range(CH):
-            ag(c, 0, l, 0, right).wait_send()
-            ag(c, 1, l, HALF, left).wait_send()
-            ag(c, 2, l, HALF, right).wait_send()
-            ag(c, 3, l, 0, left).wait_send()
-            ag(c, 4, left, 0, right).wait_send()
-            ag(c, 5, right, HALF, left).wait_send()
-        for i in range(NS):
-            rs_one(i, 0, 0, right).wait_send()
-            rs_one(i, 1, QH, left).wait_send()
-            rs_two(i, 2, 0, right, QH, right).wait_send()
-            rs_two(i, 3, 1, left, 0, left).wait_send()
-            rs_two(i, 4, 0, right, 0, right).wait_send()
-            rs_two(i, 5, 1, left, QH, left).wait_send()
-            take_all(sy, i, a2_s)
-            take_all(t, i, b2_s)
-
     prepare()
     synth_near(0)
     synth_far(0)
-    exchange(0)
-    exchange(1)
     ag_forward(1)
     synth_near(1)
     grid_stage(0)
     synth_far(1)
-    exchange(2)
     grid_stage(1)
-    exchange(3)
     scatter_start(0)
     grid_stage(2)
     scatter_middle(0)
-    scatter_start(1)
     grid_stage(3)
     sums_start()
+    scatter_start(1)
+    scatter_start(2)
     scatter_middle(1)
-    scatter_start(2)
+    reduce_middle(0)
     scatter_start(3)
     scatter_middle(2)
-    reduce_middle(0)
     sums_end()
     out0 = scatter_end(0)
     out1 = scatter_end(1)
@@ -567,10 +544,25 @@
     scatter_out(3, *out3)
     out_app = pltpu.make_async_copy(app_v, app_h, osem.at[0])
     out_app.start()
-    drain()
     reduce_middle(1)
     finish()
 
+    for c in range(CH):
+        ag(c, 0, l, 0, right).wait_send()
+        ag(c, 1, l, HALF, left).wait_send()
+        ag(c, 2, l, HALF, right).wait_send()
+        ag(c, 3, l, 0, left).wait_send()
+        ag(c, 4, left, 0, right).wait_send()
+        ag(c, 5, right, HALF, left).wait_send()
+    for i in range(NS):
+        rs_one(i, 0, 0, right).wait_send()
+        rs_one(i, 1, QH, left).wait_send()
+        rs_two(i, 2, 0, right, QH, right).wait_send()
+        rs_two(i, 3, 1, left, 0, left).wait_send()
+        rs_two(i, 4, 0, right, 0, right).wait_send()
+        rs_two(i, 5, 1, left, QH, left).wait_send()
+        take_all(sy, i, a2_s)
+        take_all(t, i, b2_s)
     for i in range(2):
         sent = v1.at[i, pl.ds(0, NO - 1)]
         pltpu.make_async_copy(sent, sent, v1_s.at[i]).wait()

time: 82.4 us -> 79.5 us (0.965)
  Pallas kernels: 81.4 us -> 78.5 us
    pallas_call x1, Pallas kernels: 79.4 us -> 76.6 us  [shards(): pl.pallas_call(kernel, out_shape=[jax.ShapeDtypeStruct(block, F32), jax.S...]
where the time goes in v4:
time: 79.5 us; the launch traced here: 79.4 us
  Pallas kernels  78.5 us (99%)
  between operations  0.87 us (1%)
    pallas_call x1, Pallas kernels, shards(): pl.pallas_call(kernel, out_shape=[jax.ShapeDtypeStruct(block, F32), jax.S...  76.6 us
    pallas_call x1, Pallas kernels, shards(): pl.pallas_call(combine, out_shape=[jax.ShapeDtypeStruct(block, F32)] * 3,...  1.97 us

profile of v4, /device:TPU:1, one launch (start us, length us, event | category | flops | bytes accessed | tf_op | source)
XLA Modules:
  0.0 79.4 jit_solution(10168176743489097610)
XLA Ops:
  0.6 0.0 copy-start.3
  0.6 0.0 copy-start.1
  0.7 0.0 copy-start
  0.7 0.0 copy-start.2
  0.7 76.6 %cg_iteration.1 = (f32[2,2,64,540]{3,2,1,0:T(8,128)S(1)}, f32[2,64,128]{2,1,0:T(8,128)S(1)}) custom-call(f32[2,2,64,540]{3,2,1,0:T(8,128)} %res_v.1, f32[2,2,64,540]{3,2,1,0:T(8,128)} %dir_v.1, f32[2,2160,512]{2,1,0:T(8,128)} %leg_h.1, s32[8,4320]{1,0:T(8,128)} %cls_h.1, s32[8,4320]{1,0:T(8,128)} %land_h.1, s32[128]{0:T(128)} %order_s.1, s32[1,128]{1,0:T(1,128)} %bitcast.2, ...), custom_call_target="tpu_custom_call" | custom-call | tf_op jit(solution)/shard_map/cg_iteration/pallas_call | solution.py:606
  77.2 0.0 copy-done.3
  77.2 0.0 copy-done.1
  77.3 0.0 copy-done
  77.3 0.0 copy-done.2
  77.3 2.0 %combine.1 = (f32[2,2,64,540]{3,2,1,0:T(8,128)}, f32[2,2,64,540]{3,2,1,0:T(8,128)}, f32[2,2,64,540]{3,2,1,0:T(8,128)}) custom-call(f32[2,2,64,540]{3,2,1,0:T(8,128)S(1)} %copy-done.2, f32[2,2,64,540]{3,2,1,0:T(8,128)S(1)} %copy-done, f32[2,2,64,540]{3,2,1,0:T(8,128)S(1)} %copy-done.1, f32[2,2,64,540]{3,2,1,0:T(8,128)S(1)} %get-tuple-element.5.app_v, ...), custom_call_target="tpu_custom_call" | custom-call | tf_op jit(solution)/shard_map/combine/pallas_call | solution.py:677
Async XLA Ops:
  0.6 76.6 %copy-start.3 = (s32[128]{0:T(128)S(1)}, s32[128]{0:T(128)}, u32[]{:S(2)}) copy-start(s32[128]{0:T(128)} %order_s.1) | copy-start | bytes 1540
  0.6 76.6 %copy-start.1 = (f32[2,2,64,540]{3,2,1,0:T(8,128)S(1)}, f32[2,2,64,540]{3,2,1,0:T(8,128)}, u32[]{:S(2)}) copy-start(f32[2,2,64,540]{3,2,1,0:T(8,128)} %dir_v.1) | copy-start | bytes 1658884
  0.7 76.6 %copy-start = (f32[2,2,64,540]{3,2,1,0:T(8,128)S(1)}, f32[2,2,64,540]{3,2,1,0:T(8,128)}, u32[]{:S(2)}) copy-start(f32[2,2,64,540]{3,2,1,0:T(8,128)} %res_v.1) | copy-start | bytes 1658884
  0.7 76.6 %copy-start.2 = (f32[2,2,64,540]{3,2,1,0:T(8,128)S(1)}, f32[2,2,64,540]{3,2,1,0:T(8,128)}, u32[]{:S(2)}) copy-start(f32[2,2,64,540]{3,2,1,0:T(8,128)} %pos_v.1) | copy-start | bytes 1658884
